TPU v7x, 128 devices: a whole 4x4x4 slice. The times are simulated.
128 devices in a mesh: tx: 4 (over z), ty: 32 (over x, y, core).
Axes of the slice: x: 4, y: 4, z: 4, core: 2. Of those that a mesh axis runs over, the one named last changes fastest.
Arguments:
- points: bfloat16 [128, 1024, 256], P(('tx', 'ty')), may hold values from -6 to 6
- counts: int32 [128], P(('tx', 'ty')), may hold values from 512 to 1024, as said below
- owner: int32 [128, 1024], P(('tx', 'ty')), may hold values from 0 to 127, as said below
- zorder: int32 [128, 2048], P(('tx', 'ty')), may hold values from 0 to 2047, as said below
- border: int32 [128, 4, 64], P(('tx', 'ty')), may hold values from 0 to 1023, as said below
- near: int32 [128, 16, 1024], P(('tx', 'ty')), may hold values from 0 to 1279, as said below
- w_near: bfloat16 [256, 256], replicated, may hold values from -0.375 to 0.375
- gain_one: float32 [256], replicated, may hold values from 0.1 to 1.9
- conv_w: bfloat16 [3, 8, 32, 32], replicated, may hold values from -0.625 to 0.625
- gain_two: float32 [256], replicated, may hold values from 0.1 to 1.9
- w_up: bfloat16 [256, 1024], replicated, may hold values from -0.375 to 0.375
- w_down: bfloat16 [1024, 256], replicated, may hold values from -0.1875 to 0.1875
- grad_out: bfloat16 [128, 1024, 256], P(('tx', 'ty')), may hold values from -6 to 6
Outputs:
- out_rows: bfloat16 [128, 1024, 256], P(('tx', 'ty'))
- grad_points: bfloat16 [128, 1024, 256], P(('tx', 'ty'))
- grad_w_near: float32 [256, 256], replicated
- grad_gain_one: float32 [256], replicated
- grad_conv: float32 [3, 8, 32, 32], replicated
- grad_gain_two: float32 [256], replicated
- grad_w_up: float32 [256, 1024], replicated
- grad_w_down: float32 [1024, 256], replicated
Inputs may be any that keep to these rules, and one draw needn't show every extreme that they name: `counts`: every tile has at least half of its slots live, and some tile has all of them live. Only live rows count. Among the live rows of one tile at most 16 name the same owner. One particular owner receives exactly 16 live rows from every tile; every other owner receives at most 16 live rows from each tile, so its receive buffer may be partly empty. `zorder`: each owner's entry is a permutation of its 2048 receive slots whose first entries name exactly the filled slots. `border`: each list names distinct live rows of its tile; lists toward a side outside the grid are never read. `near`: indices below 1024 name live rows of the tile; the others name halo rows of blocks whose neighbour tile exists.
All inputs are finite; a program needn't handle non-finite values.
Results may differ from a plain program's by a relative error of at most 0.015.
Values may be sent and summed in bfloat16 or wider, within the bound.
A program may use at most 64 MiB of HBM per device.

v0:
```python
import math

import jax
import jax.numpy as jnp
from jax import lax
from jax.sharding import PartitionSpec as P

PATCH = 1024


eps_norm = 1e-06
gelu_coef = 0.7978845608028654
cubic_coef = 0.044715


def shifted(value, axis, steps):
    count = lax.axis_size(axis)
    initial, last = (max(0, -steps), min(count, count - steps))
    return lax.ppermute(value, axis, [(source, source + steps) for source in range(initial, last)])


def gelu_tanh(value):
    inner = gelu_coef * (value + cubic_coef * value * value * value)
    return 0.5 * value * (1.0 + jnp.tanh(inner))


def gelu_slope(value):
    inner = gelu_coef * (value + cubic_coef * value * value * value)
    tangent = jnp.tanh(inner)
    return 0.5 * (1.0 + tangent) + 0.5 * value * (1.0 - tangent * tangent) * gelu_coef * (
        1.0 + 3.0 * cubic_coef * value * value
    )


def inverse_rms(value):
    return lax.rsqrt(jnp.mean(value * value, axis=-1, keepdims=True) + eps_norm)


def tile_forward(points_tile, halo_rows, near_tile, w_near):
    extended = jnp.concatenate([points_tile, halo_rows], axis=0)
    count_near = near_tile.shape[0]

    def add_neighbour(index, total):
        return total + jnp.take(extended, near_tile[index], axis=0).astype(jnp.float32)

    total = lax.fori_loop(0, count_near, add_neighbour, jnp.zeros(points_tile.shape, jnp.float32))
    average = (total * (1.0 / count_near)).astype(jnp.bfloat16)
    linear_part = jnp.dot(average, w_near, preferred_element_type=jnp.float32)
    lifted = (points_tile.astype(jnp.float32) + gelu_tanh(linear_part)).astype(jnp.bfloat16)
    return (average, linear_part, lifted)


def tile_backward(lifted_grad, average, linear_part, near_tile, w_near, ext_count):
    count_near = near_tile.shape[0]
    tile_rows = lifted_grad.shape[0]
    act_grad = (lifted_grad.astype(jnp.float32) * gelu_slope(linear_part)).astype(jnp.bfloat16)
    near_grad = lax.dot_general(
        average, act_grad, (((0,), (0,)), ((), ())), preferred_element_type=jnp.float32
    )
    spread = lax.dot_general(
        act_grad, w_near, (((1,), (1,)), ((), ())), preferred_element_type=jnp.float32
    ) * (1.0 / count_near)

    def scatter_neighbour(index, total):
        return total.at[near_tile[index]].add(spread)

    ext_grad = lax.fori_loop(
        0, count_near, scatter_neighbour, jnp.zeros((ext_count, spread.shape[1]), jnp.float32)
    )
    row_grad = lifted_grad.astype(jnp.float32) + ext_grad[:tile_rows]
    halo_grad = ext_grad[tile_rows:].astype(jnp.bfloat16)
    return (near_grad, row_grad, halo_grad)


def route_ranks(owner_tile, count, tiles):
    tile_rows = owner_tile.shape[0]
    index = jnp.arange(tile_rows, dtype=jnp.int32)
    live = index < count
    score = jnp.where(live, owner_tile * tile_rows + index, tiles * tile_rows + index)
    order = jnp.argsort(score, stable=True)
    members = (owner_tile[:, None] == jnp.arange(tiles, dtype=jnp.int32)[None, :]) & live[:, None]
    per_owner = jnp.sum(members.astype(jnp.int32), axis=0)
    starts = jnp.cumsum(per_owner) - per_owner
    sorted_owner = jnp.take(owner_tile, order)
    ranked = index - jnp.take(starts, sorted_owner)
    rank = jnp.zeros((tile_rows,), jnp.int32).at[order].set(ranked)
    return (rank, live)


def shift_down(rows):
    return jnp.concatenate([jnp.zeros_like(rows[:1]), rows[:-1]], axis=0)


def shift_up(rows):
    return jnp.concatenate([rows[1:], jnp.zeros_like(rows[:1])], axis=0)


def block_taps(conv_w):
    groups, inner = (conv_w.shape[1], conv_w.shape[2])
    identity_blocks = jnp.eye(groups, dtype=conv_w.dtype)
    full = jnp.einsum("gh,ogab->ogahb", identity_blocks, conv_w)
    return full.reshape(conv_w.shape[0], groups * inner, groups * inner)


def grouped_weight(inputs, outputs, groups, inner):
    length = inputs.shape[0]
    left = inputs.reshape(length, groups, inner)
    right = outputs.reshape(length, groups, inner)
    return jnp.einsum("pga,pgb->gab", left, right, preferred_element_type=jnp.float32)


def tap_back(rows, tap):
    return lax.dot_general(rows, tap, (((1,), (1,)), ((), ())), preferred_element_type=jnp.float32)


def patch_pass(serial, out_grad, gain_one, conv_w, taps_full, gain_two, w_up, w_down):
    groups, inner = (conv_w.shape[1], conv_w.shape[2])
    serial_f = serial.astype(jnp.float32)
    scale_one = inverse_rms(serial_f)
    normed = (serial_f * scale_one * gain_one).astype(jnp.bfloat16)
    taps = (shift_down(normed), normed, shift_up(normed))
    mixed = (
        jnp.dot(taps[0], taps_full[0], preferred_element_type=jnp.float32)
        + jnp.dot(taps[1], taps_full[1], preferred_element_type=jnp.float32)
        + jnp.dot(taps[2], taps_full[2], preferred_element_type=jnp.float32)
    )
    state = serial_f + mixed
    scale_two = inverse_rms(state)
    second = (state * scale_two * gain_two).astype(jnp.bfloat16)
    hidden_pre = jnp.dot(second, w_up, preferred_element_type=jnp.float32)
    hidden = gelu_tanh(hidden_pre).astype(jnp.bfloat16)
    result = (state + jnp.dot(hidden, w_down, preferred_element_type=jnp.float32)).astype(
        jnp.bfloat16
    )
    down_grad = lax.dot_general(
        hidden, out_grad, (((0,), (0,)), ((), ())), preferred_element_type=jnp.float32
    )
    hidden_grad = lax.dot_general(
        out_grad, w_down, (((1,), (1,)), ((), ())), preferred_element_type=jnp.float32
    ).astype(jnp.bfloat16)
    pre_grad = (hidden_grad.astype(jnp.float32) * gelu_slope(hidden_pre)).astype(jnp.bfloat16)
    up_grad = lax.dot_general(
        second, pre_grad, (((0,), (0,)), ((), ())), preferred_element_type=jnp.float32
    )
    second_grad = lax.dot_general(
        pre_grad, w_up, (((1,), (1,)), ((), ())), preferred_element_type=jnp.float32
    ).astype(jnp.bfloat16)
    unit_two = state * scale_two
    weighted_two = second_grad.astype(jnp.float32) * gain_two
    gain_two_grad = jnp.sum(second_grad.astype(jnp.float32) * unit_two, axis=0)
    state_grad = out_grad.astype(jnp.float32) + scale_two * (
        weighted_two - unit_two * jnp.mean(weighted_two * unit_two, axis=-1, keepdims=True)
    )
    mixed_grad = state_grad.astype(jnp.bfloat16)
    conv_grad = jnp.stack(
        [
            grouped_weight(taps[0], mixed_grad, groups, inner),
            grouped_weight(taps[1], mixed_grad, groups, inner),
            grouped_weight(taps[2], mixed_grad, groups, inner),
        ],
        axis=0,
    )
    normed_grad = (
        shift_up(tap_back(mixed_grad, taps_full[0]))
        + tap_back(mixed_grad, taps_full[1])
        + shift_down(tap_back(mixed_grad, taps_full[2]))
    ).astype(jnp.bfloat16)
    unit_one = serial_f * scale_one
    weighted_one = normed_grad.astype(jnp.float32) * gain_one
    gain_one_grad = jnp.sum(normed_grad.astype(jnp.float32) * unit_one, axis=0)
    serial_grad = (
        state_grad
        + scale_one
        * (weighted_one - unit_one * jnp.mean(weighted_one * unit_one, axis=-1, keepdims=True))
    ).astype(jnp.bfloat16)
    return (result, serial_grad, (gain_one_grad, conv_grad, gain_two_grad, up_grad, down_grad))


def pass_columns(rows, shift_by):
    return shifted(rows, "tx", shift_by)


def pass_lines(rows, shift_by):
    return shifted(rows, "ty", shift_by)


def body(
    points,
    counts,
    owner,
    zorder,
    border,
    near,
    w_near,
    gain_one,
    conv_w,
    gain_two,
    w_up,
    w_down,
    grad_out,
):
    points_tile = points[0]
    tile_rows, width = points_tile.shape
    lists = border[0]
    border_rows = lists.shape[1]
    cols_count = lax.axis_size("tx")
    lines_count = lax.axis_size("ty")
    tiles = cols_count * lines_count
    recv_rows = zorder.shape[1]
    capacity = recv_rows // tiles
    near_tile = near[0]
    owner_tile = owner[0]
    sent = jnp.take(points_tile, lists.reshape(-1), axis=0).reshape(4, border_rows, width)
    halo = jnp.concatenate(
        [
            pass_columns(sent[0], -1),
            pass_columns(sent[1], 1),
            pass_lines(sent[2], -1),
            pass_lines(sent[3], 1),
        ],
        axis=0,
    )
    average, linear_part, lifted = tile_forward(points_tile, halo, near_tile, w_near)
    rank, live = route_ranks(owner_tile, counts[0], tiles)
    slots = jnp.where(live, owner_tile * capacity + rank, tiles * capacity)
    payload = jnp.concatenate([lifted, grad_out[0]], axis=1)
    outgoing = (
        jnp.zeros((tiles * capacity, 2 * width), jnp.bfloat16).at[slots].set(payload, mode="drop")
    )
    incoming = lax.all_to_all(outgoing, ("tx", "ty"), split_axis=0, concat_axis=0, tiled=True)
    serial_both = jnp.take(incoming, zorder[0], axis=0)
    taps_full = block_taps(conv_w)
    zero_sums = (
        jnp.zeros((width,), jnp.float32),
        jnp.zeros(conv_w.shape, jnp.float32),
        jnp.zeros((width,), jnp.float32),
        jnp.zeros(w_up.shape, jnp.float32),
        jnp.zeros(w_down.shape, jnp.float32),
    )

    def patch_step(carry, block):
        result, serial_grad, grads = patch_pass(
            block[:, :width], block[:, width:], gain_one, conv_w, taps_full, gain_two, w_up, w_down
        )
        return (jax.tree.map(lambda left, right: left + right, carry, grads), (result, serial_grad))

    sums, (results, serial_grads) = lax.scan(
        patch_step, zero_sums, serial_both.reshape(recv_rows // PATCH, PATCH, 2 * width)
    )
    back = jnp.concatenate(
        [results.reshape(recv_rows, width), serial_grads.reshape(recv_rows, width)], axis=1
    )
    back_slots = jnp.zeros_like(back).at[zorder[0]].set(back)
    returned = lax.all_to_all(back_slots, ("tx", "ty"), split_axis=0, concat_axis=0, tiled=True)
    back_rows = jnp.take(returned, slots, axis=0, mode="fill", fill_value=0)
    out_rows = back_rows[:, :width]
    lifted_grad = back_rows[:, width:]
    near_grad, row_grad, halo_grad = tile_backward(
        lifted_grad, average, linear_part, near_tile, w_near, tile_rows + 4 * border_rows
    )
    came_back = (
        pass_columns(halo_grad[0:border_rows], 1),
        pass_columns(halo_grad[border_rows : 2 * border_rows], -1),
        pass_lines(halo_grad[2 * border_rows : 3 * border_rows], 1),
        pass_lines(halo_grad[3 * border_rows : 4 * border_rows], -1),
    )
    for direction in range(4):
        row_grad = row_grad.at[lists[direction]].add(came_back[direction].astype(jnp.float32))
    near_sum, gain_one_sum, conv_sum, gain_two_sum, up_sum, down_sum = lax.psum(
        (near_grad, sums[0], sums[1], sums[2], sums[3], sums[4]), ("tx", "ty")
    )
    totals = (gain_one_sum, conv_sum, gain_two_sum, up_sum, down_sum)
    scale = 1.0 / math.sqrt(tiles * tile_rows)
    return (
        out_rows[None],
        row_grad.astype(jnp.bfloat16)[None],
        near_sum * scale,
        totals[0] * scale,
        totals[1] * scale,
        totals[2] * scale,
        totals[3] * scale,
        totals[4] * scale,
    )


def solution(mesh):
    placed = (
        P(("tx", "ty"), None, None),
        P(("tx", "ty")),
        P(("tx", "ty"), None),
        P(("tx", "ty"), None),
        P(("tx", "ty"), None, None),
        P(("tx", "ty"), None, None),
        P(),
        P(),
        P(),
        P(),
        P(),
        P(),
        P(("tx", "ty"), None, None),
    )
    return jax.shard_map(
        body,
        mesh=mesh,
        in_specs=placed,
        out_specs=(
            P(("tx", "ty"), None, None),
            P(("tx", "ty"), None, None),
            P(),
            P(),
            P(),
            P(),
            P(),
            P(),
        ),
        check_vma=False,
    )
```

profile of v0, /device:TPU:1, one launch (start us, length us, event | category | flops | bytes accessed | tf_op | source)
XLA Modules:
  0.0 547.0 jit_solution(10170970694803453524)
XLA Ops:
  11.1 4.6 collective-permute-start.3
  17.6 3.5 collective-permute-start.1
  24.9 4.4 sort.17
  29.3 4.5 gather_fusion.1
  34.2 6.6 %gather_fusion.2 = s32[1024]{0:T(1024)S(1)} fusion(s32[128]{0:T(128)S(1)} %sub.18, s32[1024]{0:T(1024)S(1)} %broadcast_clamp_fusion.3), kind=kCustom, calls=%fused_computation.2 | custom fusion | bytes 12288 | tf_op jit(solution)/shard_map/jit(_take)/gather | solution.py:85
  40.8 4.3 scatter_custom_fusion.1
  49.6 81.9 %while.51 = (s32[]{:T(128)}, f32[1024,256]{1,0:T(8,128)S(1)}, s32[16,1024]{1,0:T(8,128)}, bf16[1280,256]{1,0:T(8,128)(2,1)S(1)}, s32[]{:T(128)}, /*index=5*/s32[]{:T(128)}) while((s32[]{:T(128)}, f32[1024,256]{1,0:T(8,128)S(1)}, s32[16,1024]{1,0:T(8,128)}, bf16[1280,256]{1,0:T(8,128)(2,1)S(1)}, s32[]{:T(128)}, ...), condition=%wide.region_5.6_spmd.clone, body=%wide.region_4.5_spmd.clone.sunk | while | flops 1058819 | bytes 3700827 | solution.py:46
  50.5 3.9 gather_fusion
  55.6 3.9 gather_fusion
  60.7 3.9 gather_fusion
  65.8 3.9 gather_fusion
  70.9 3.9 gather_fusion
  76.0 3.9 gather_fusion
  81.2 3.9 gather_fusion
  86.3 3.9 gather_fusion
  91.4 3.9 gather_fusion
  96.5 3.9 gather_fusion
  101.6 3.9 gather_fusion
  106.7 3.9 gather_fusion
  111.9 3.9 gather_fusion
  117.0 3.9 gather_fusion
  122.1 3.9 gather_fusion
  127.2 3.9 gather_fusion
  133.7 6.7 %scatter_custom_fusion.2 = bf16[2048,512]{1,0:T(8,128)(2,1)} fusion(s32[1024]{0:T(1024)S(1)} %get-tuple-element.408, bf16[1024,512]{1,0:T(8,128)(2,1)S(1)} %copy.65, bf16[]{:T(256)} %constant.215.clone.1), kind=kCustom, calls=%fused_computation.126 | custom fusion | bytes 2097154 | tf_op jit(solution)/shard_map/scatter | solution.py:228
  140.4 22.0 %all-to-all-start = ((bf16[128,16,512]{2,1,0:T(8,128)(2,1)}), bf16[128,16,512]{2,1,0:T(8,128)(2,1)S(1)}, u32[]{:S(2)}, u32[]{:S(2)}) async-start(bf16[128,16,512]{2,1,0:T(8,128)(2,1)} %bitcast.194), calls=%async_computation | async-start | bytes 4194304 | tf_op jit(solution)/shard_map/all_to_all | solution.py:230
  163.7 2.3 multiply_bitcast_fusion
  166.0 3.0 reshape.393
  169.1 23.7 %all-to-all-done = bf16[128,16,512]{2,1,0:T(8,128)(2,1)S(1)} async-done(((bf16[128,16,512]{2,1,0:T(8,128)(2,1)}), bf16[128,16,512]{2,1,0:T(8,128)(2,1)S(1)}, u32[]{:S(2)}, u32[]{:S(2)}) %all-to-all-start) | async-done | bytes 2097184 | tf_op jit(solution)/shard_map/all_to_all | solution.py:230
  192.8 9.2 %gather_fusion.4 = bf16[2048,512]{1,0:T(8,128)(2,1)} fusion(bf16[2048,512]{1,0:T(8,128)(2,1)S(1)} %bitcast.188, s32[2048]{0:T(1024)S(1)} %broadcast_clamp_fusion.1), kind=kCustom, calls=%fused_computation.4 | custom fusion | bytes 4202496 | tf_op jit(solution)/shard_map/jit(_take)/gather | solution.py:231
  202.0 3.0 copy.66
  206.6 68.3 %while.52 = (s32[]{:T(128)}, f32[256]{0:T(256)S(1)}, f32[3,8,32,32]{3,2,1,0:T(8,128)}, f32[256]{0:T(256)S(1)}, f32[256,1024]{1,0:T(8,128)}, /*index=5*/f32[1024,...) while((s32[]{:T(128)}, f32[256]{0:T(256)S(1)}, ...), condition=%wide.region_14.15_spmd.clone, body=%wide.region_7.14_spmd.clone.sunk | while | flops 4135946752 | bytes 123703776 | solution.py:247
  218.0 2.5 fusion.180
  221.8 4.9 convolution_add_fusion.11
  226.7 3.0 fusion.173
  252.0 2.5 fusion.180
  255.8 5.2 convolution_add_fusion.11
  261.0 3.0 fusion.173
  274.9 11.5 %scatter_custom_fusion.3 = bf16[2048,512]{1,0:T(8,128)(2,1)} fusion(s32[2048]{0:T(1024)} %bitcast.205, bf16[2048,256]{1,0:T(8,128)(2,1)} %bitcast.198, bf16[]{:T(256)} %constant.244, bf16[2048,256]{1,0:T(8,128)(2,1)} %bitcast.199, bf16[]{:T(256)} %constant.215.clone.1), kind=kCustom, calls=%fused_computation.105 | custom fusion | flops 4194304 | bytes 4195328 | tf_op jit(solution)/shard_map/scatter | solution.py:253
  286.4 4.3 all-to-all-start.1
  291.3 81.3 %all-reduce.4 = (f32[256]{0:T(256)S(1)}, f32[256]{0:T(256)S(1)}) all-reduce(f32[256]{0:T(256)S(1)} %get-tuple-element.250, f32[256]{0:T(256)S(1)} %get-tuple-element.252), channel_id=1, replica_groups=mesh['tx'=4,'ty'=32] {'tx','ty'}, use_global_device_ids=true, to_apply=%region_24.25 | all-reduce | flops 512 | bytes 4096 | tf_op jit(solution)/shard_map/psum | solution.py:269
  373.2 4.0 gather_fusion.5
  381.2 117.5 %while.50 = (s32[]{:T(128)}, f32[1280,256]{1,0:T(8,128)S(1)}, s32[16,1024]{1,0:T(8,128)}, f32[1024,256]{1,0:T(8,128)S(1)}, s32[]{:T(128)}) while((s32[]{:T(128)}, f32[1280,256]{1,0:T(8,128)S(1)}, s32[16,1024]{1,0:T(8,128)}, f32[1024,256]{1,0:T(8,128)S(1)}, s32[]{:T(128)}) %tuple.124), condition=%wide.region_18.19_spmd, body=%wide.region_16.18_spmd.sunk | while | flops 265218 | bytes 3158089 | solution.py:67
  382.0 6.5 %scatter_fusion = f32[1280,256]{1,0:T(8,128)S(1)} fusion(f32[1280,256]{1,0:T(8,128)S(1)} %get-tuple-element.679, s32[1024]{0:T(1024)S(1)} %bitcast.200, f32[1024,256]{1,0:T(8,128)S(1)} %get-tuple-element.686), kind=kCustom, calls=%fused_computation.6.clone.1 | custom fusion | flops 262144 | bytes 3149824 | tf_op jit(solution)/shard_map/while/body/eval_jaxpr/scatter-add | solution.py:65
  389.4 6.5 %scatter_fusion = f32[1280,256]{1,0:T(8,128)S(1)} fusion(f32[1280,256]{1,0:T(8,128)S(1)} %get-tuple-element.679, s32[1024]{0:T(1024)S(1)} %bitcast.200, f32[1024,256]{1,0:T(8,128)S(1)} %get-tuple-element.686), kind=kCustom, calls=%fused_computation.6.clone.1 | custom fusion | flops 262144 | bytes 3149824 | tf_op jit(solution)/shard_map/while/body/eval_jaxpr/scatter-add | solution.py:65
  396.7 6.5 %scatter_fusion = f32[1280,256]{1,0:T(8,128)S(1)} fusion(f32[1280,256]{1,0:T(8,128)S(1)} %get-tuple-element.679, s32[1024]{0:T(1024)S(1)} %bitcast.200, f32[1024,256]{1,0:T(8,128)S(1)} %get-tuple-element.686), kind=kCustom, calls=%fused_computation.6.clone.1 | custom fusion | flops 262144 | bytes 3149824 | tf_op jit(solution)/shard_map/while/body/eval_jaxpr/scatter-add | solution.py:65
  404.1 6.5 %scatter_fusion = f32[1280,256]{1,0:T(8,128)S(1)} fusion(f32[1280,256]{1,0:T(8,128)S(1)} %get-tuple-element.679, s32[1024]{0:T(1024)S(1)} %bitcast.200, f32[1024,256]{1,0:T(8,128)S(1)} %get-tuple-element.686), kind=kCustom, calls=%fused_computation.6.clone.1 | custom fusion | flops 262144 | bytes 3149824 | tf_op jit(solution)/shard_map/while/body/eval_jaxpr/scatter-add | solution.py:65
  411.4 6.5 %scatter_fusion = f32[1280,256]{1,0:T(8,128)S(1)} fusion(f32[1280,256]{1,0:T(8,128)S(1)} %get-tuple-element.679, s32[1024]{0:T(1024)S(1)} %bitcast.200, f32[1024,256]{1,0:T(8,128)S(1)} %get-tuple-element.686), kind=kCustom, calls=%fused_computation.6.clone.1 | custom fusion | flops 262144 | bytes 3149824 | tf_op jit(solution)/shard_map/while/body/eval_jaxpr/scatter-add | solution.py:65
  418.7 6.5 %scatter_fusion = f32[1280,256]{1,0:T(8,128)S(1)} fusion(f32[1280,256]{1,0:T(8,128)S(1)} %get-tuple-element.679, s32[1024]{0:T(1024)S(1)} %bitcast.200, f32[1024,256]{1,0:T(8,128)S(1)} %get-tuple-element.686), kind=kCustom, calls=%fused_computation.6.clone.1 | custom fusion | flops 262144 | bytes 3149824 | tf_op jit(solution)/shard_map/while/body/eval_jaxpr/scatter-add | solution.py:65
  426.1 6.5 %scatter_fusion = f32[1280,256]{1,0:T(8,128)S(1)} fusion(f32[1280,256]{1,0:T(8,128)S(1)} %get-tuple-element.679, s32[1024]{0:T(1024)S(1)} %bitcast.200, f32[1024,256]{1,0:T(8,128)S(1)} %get-tuple-element.686), kind=kCustom, calls=%fused_computation.6.clone.1 | custom fusion | flops 262144 | bytes 3149824 | tf_op jit(solution)/shard_map/while/body/eval_jaxpr/scatter-add | solution.py:65
  433.4 6.5 %scatter_fusion = f32[1280,256]{1,0:T(8,128)S(1)} fusion(f32[1280,256]{1,0:T(8,128)S(1)} %get-tuple-element.679, s32[1024]{0:T(1024)S(1)} %bitcast.200, f32[1024,256]{1,0:T(8,128)S(1)} %get-tuple-element.686), kind=kCustom, calls=%fused_computation.6.clone.1 | custom fusion | flops 262144 | bytes 3149824 | tf_op jit(solution)/shard_map/while/body/eval_jaxpr/scatter-add | solution.py:65
  440.8 6.5 %scatter_fusion = f32[1280,256]{1,0:T(8,128)S(1)} fusion(f32[1280,256]{1,0:T(8,128)S(1)} %get-tuple-element.679, s32[1024]{0:T(1024)S(1)} %bitcast.200, f32[1024,256]{1,0:T(8,128)S(1)} %get-tuple-element.686), kind=kCustom, calls=%fused_computation.6.clone.1 | custom fusion | flops 262144 | bytes 3149824 | tf_op jit(solution)/shard_map/while/body/eval_jaxpr/scatter-add | solution.py:65
  448.1 6.5 %scatter_fusion = f32[1280,256]{1,0:T(8,128)S(1)} fusion(f32[1280,256]{1,0:T(8,128)S(1)} %get-tuple-element.679, s32[1024]{0:T(1024)S(1)} %bitcast.200, f32[1024,256]{1,0:T(8,128)S(1)} %get-tuple-element.686), kind=kCustom, calls=%fused_computation.6.clone.1 | custom fusion | flops 262144 | bytes 3149824 | tf_op jit(solution)/shard_map/while/body/eval_jaxpr/scatter-add | solution.py:65
  455.5 6.5 %scatter_fusion = f32[1280,256]{1,0:T(8,128)S(1)} fusion(f32[1280,256]{1,0:T(8,128)S(1)} %get-tuple-element.679, s32[1024]{0:T(1024)S(1)} %bitcast.200, f32[1024,256]{1,0:T(8,128)S(1)} %get-tuple-element.686), kind=kCustom, calls=%fused_computation.6.clone.1 | custom fusion | flops 262144 | bytes 3149824 | tf_op jit(solution)/shard_map/while/body/eval_jaxpr/scatter-add | solution.py:65
  462.8 6.5 %scatter_fusion = f32[1280,256]{1,0:T(8,128)S(1)} fusion(f32[1280,256]{1,0:T(8,128)S(1)} %get-tuple-element.679, s32[1024]{0:T(1024)S(1)} %bitcast.200, f32[1024,256]{1,0:T(8,128)S(1)} %get-tuple-element.686), kind=kCustom, calls=%fused_computation.6.clone.1 | custom fusion | flops 262144 | bytes 3149824 | tf_op jit(solution)/shard_map/while/body/eval_jaxpr/scatter-add | solution.py:65
  470.1 6.5 %scatter_fusion = f32[1280,256]{1,0:T(8,128)S(1)} fusion(f32[1280,256]{1,0:T(8,128)S(1)} %get-tuple-element.679, s32[1024]{0:T(1024)S(1)} %bitcast.200, f32[1024,256]{1,0:T(8,128)S(1)} %get-tuple-element.686), kind=kCustom, calls=%fused_computation.6.clone.1 | custom fusion | flops 262144 | bytes 3149824 | tf_op jit(solution)/shard_map/while/body/eval_jaxpr/scatter-add | solution.py:65
  477.5 6.5 %scatter_fusion = f32[1280,256]{1,0:T(8,128)S(1)} fusion(f32[1280,256]{1,0:T(8,128)S(1)} %get-tuple-element.679, s32[1024]{0:T(1024)S(1)} %bitcast.200, f32[1024,256]{1,0:T(8,128)S(1)} %get-tuple-element.686), kind=kCustom, calls=%fused_computation.6.clone.1 | custom fusion | flops 262144 | bytes 3149824 | tf_op jit(solution)/shard_map/while/body/eval_jaxpr/scatter-add | solution.py:65
  484.8 6.5 %scatter_fusion = f32[1280,256]{1,0:T(8,128)S(1)} fusion(f32[1280,256]{1,0:T(8,128)S(1)} %get-tuple-element.679, s32[1024]{0:T(1024)S(1)} %bitcast.200, f32[1024,256]{1,0:T(8,128)S(1)} %get-tuple-element.686), kind=kCustom, calls=%fused_computation.6.clone.1 | custom fusion | flops 262144 | bytes 3149824 | tf_op jit(solution)/shard_map/while/body/eval_jaxpr/scatter-add | solution.py:65
  492.2 6.5 %scatter_fusion = f32[1280,256]{1,0:T(8,128)S(1)} fusion(f32[1280,256]{1,0:T(8,128)S(1)} %get-tuple-element.679, s32[1024]{0:T(1024)S(1)} %bitcast.200, f32[1024,256]{1,0:T(8,128)S(1)} %get-tuple-element.686), kind=kCustom, calls=%fused_computation.6.clone.1 | custom fusion | flops 262144 | bytes 3149824 | tf_op jit(solution)/shard_map/while/body/eval_jaxpr/scatter-add | solution.py:65
  500.3 2.5 collective-permute-start.7
  502.8 3.4 collective-permute-start.6
  507.5 4.0 collective-permute-start.4
  520.6 11.0 %all-reduce.8.cloned.1.call-done = (f32[256,256]{1,0:T(8,128)}, f32[3,8,32,32]{3,2,1,0:T(8,128)}, f32[256,1024]{1,0:T(8,128)}, f32[1024,256]{1,0:T(8,128)}) async-done(((f32[256,256]{1,0:T(8,128)}, f32[3,8,32,32]{3,2,1,0:T(8,128)}, f32[256,1024]{1,0:T(8,128)}, f32[1024,256]{1,0:T(8,128)}), (f32[256,256]{1,0:T(8,128)}, f32[3,8,32,32]{3,2,1,0:T(8,128)}, f32[256,1024]{1,0:T(8,128)}, ...) | async-done | bytes 2457616 | tf_op jit(solution)/shard_map/psum | solution.py:269
  535.1 2.3 broadcast_multiply_fusion.3
  537.5 2.3 broadcast_multiply_fusion.2
  (297 shorter events, 116.2 us)
Async XLA Ops:
  7.2 124.4 %copy-start = (bf16[256,256]{1,0:T(8,128)(2,1)S(1)}, bf16[256,256]{1,0:T(8,128)(2,1)}, u32[]{:S(2)}) copy-start(bf16[256,256]{1,0:T(8,128)(2,1)} %param.25) | copy-start | bytes 393220
  7.2 22.1 %copy-start.1 = (s32[1,1024]{1,0:T(1,128)S(1)}, s32[1,1024]{1,0:T(1,128)}, u32[]{:S(2)}) copy-start(s32[1,1024]{1,0:T(1,128)} %param.21) | copy-start | bytes 12292
  11.1 35.9 %collective-permute-start.3 = (bf16[64,256]{0,1:T(8,128)(2,1)S(1)}, bf16[64,256]{0,1:T(8,128)(2,1)S(1)}, u32[]{:S(2)}, u32[]{:S(2)}) collective-permute-start(bf16[64,256]{0,1:T(8,128)(2,1)S(1)} %get-tuple-element.423), channel_id=1, source_target_pairs={{0,1},{1,2},{2,3},{3,4},{4,5},{5,6},{6,7},{7,8},{8,9},{9,10},{10,1... | collective-permute-start | bytes 98312 | tf_op jit(solution)/shard_map/ppermute | solution.py:19
  15.7 31.3 %collective-permute-start.2 = (bf16[64,256]{0,1:T(8,128)(2,1)S(1)}, bf16[64,256]{0,1:T(8,128)(2,1)S(1)}, u32[]{:S(2)}, u32[]{:S(2)}) collective-permute-start(bf16[64,256]{0,1:T(8,128)(2,1)S(1)} %get-tuple-element.424), channel_id=1, source_target_pairs={{1,0},{2,1},{3,2},{4,3},{5,4},{6,5},{7,6},{8,7},{9,8},{10,9},{11,1... | collective-permute-start | bytes 98312 | tf_op jit(solution)/shard_map/ppermute | solution.py:19
  17.6 29.4 %collective-permute-start.1 = (bf16[64,256]{0,1:T(8,128)(2,1)S(1)}, bf16[64,256]{0,1:T(8,128)(2,1)S(1)}, u32[]{:S(2)}, u32[]{:S(2)}) collective-permute-start(bf16[64,256]{0,1:T(8,128)(2,1)S(1)} %get-tuple-element.425), channel_id=1, source_target_pairs={{0,32},{32,64},{64,96},{1,33},{33,65},{65,97},{2,34},{34,66},{66,9... | collective-permute-start | bytes 98312 | tf_op jit(solution)/shard_map/ppermute | solution.py:19
  21.2 25.8 %collective-permute-start = (bf16[64,256]{0,1:T(8,128)(2,1)S(1)}, bf16[64,256]{0,1:T(8,128)(2,1)S(1)}, u32[]{:S(2)}, u32[]{:S(2)}) collective-permute-start(bf16[64,256]{0,1:T(8,128)(2,1)S(1)} %get-tuple-element.426), channel_id=1, source_target_pairs={{32,0},{64,32},{96,64},{33,1},{65,33},{97,65},{34,2},{66,34},{98,6... | collective-permute-start | bytes 98312 | tf_op jit(solution)/shard_map/ppermute | solution.py:19
  29.3 16.5 %copy-start.12 = (bf16[1,1024,256]{2,1,0:T(8,128)(2,1)S(1)}, bf16[1,1024,256]{2,1,0:T(8,128)(2,1)}, u32[]{:S(2)}) copy-start(bf16[1,1024,256]{2,1,0:T(8,128)(2,1)} %param.19) | copy-start | bytes 1572868
  29.3 16.7 %copy-start.14 = (bf16[1,1024,256]{2,1,0:T(8,128)(2,1)S(1)}, bf16[1,1024,256]{2,1,0:T(8,128)(2,1)}, u32[]{:S(2)}) copy-start(bf16[1,1024,256]{2,1,0:T(8,128)(2,1)} %param.31) | copy-start | bytes 1572868
  45.7 87.9 %copy-start.24 = (s32[1024]{0:T(1024)}, s32[1024]{0:T(1024)S(1)}, u32[]{:S(2)}) copy-start(s32[1024]{0:T(1024)S(1)} %get-tuple-element.408) | copy-start | bytes 12292
  47.0 0.6 copy-start.17
  47.0 0.6 copy-start.18
  47.0 0.6 copy-start.19
  47.7 0.6 copy-start.20
  49.6 83.5 %copy-start.13 = (bf16[1,1024,256]{1,2,0:T(8,128)(2,1)S(1)}, bf16[1,1024,256]{1,2,0:T(8,128)(2,1)}, u32[]{:S(2)}) copy-start(bf16[1,1024,256]{1,2,0:T(8,128)(2,1)} %copy.64) | copy-start | bytes 1572868
  131.5 8.9 %copy-start.6 = (f32[1024,256]{1,0:T(8,128)}, f32[1024,256]{1,0:T(8,128)S(1)}, u32[]{:S(2)}) copy-start(f32[1024,256]{1,0:T(8,128)S(1)} %get-tuple-element.246) | copy-start | bytes 3145732
  133.1 29.9 %copy-start.21 = (s32[1,2048]{1,0:T(1,128)S(1)}, s32[1,2048]{1,0:T(1,128)}, u32[]{:S(2)}) copy-start(s32[1,2048]{1,0:T(1,128)} %param.22) | copy-start | bytes 24580
  140.4 52.4 %all-to-all-start = ((bf16[128,16,512]{2,1,0:T(8,128)(2,1)}), bf16[128,16,512]{2,1,0:T(8,128)(2,1)S(1)}, u32[]{:S(2)}, u32[]{:S(2)}) async-start(bf16[128,16,512]{2,1,0:T(8,128)(2,1)} %bitcast.194), calls=%async_computation | async-start | bytes 4194304 | tf_op jit(solution)/shard_map/all_to_all | solution.py:230
  169.1 32.9 %copy-start.22 = (s32[2048,1]{0,1:T(1,128)}, s32[2048,1]{0,1:T(1,128)S(1)}, u32[]{:S(2)}) copy-start(s32[2048,1]{0,1:T(1,128)S(1)} %compare_select_fusion.3) | copy-start | bytes 24580
  202.0 4.6 copy-start.15
  202.0 4.6 copy-start.16
  213.4 4.7 copy-start.27
  216.1 1.9 copy-start.2
  221.8 4.9 copy-start.3
  221.8 4.9 copy-start.28
  229.8 2.1 copy-start.8
  231.9 1.3 copy-start.4
  231.9 1.9 copy-start.5
  232.8 3.0 copy-start.9
  232.8 1.3 copy-start.10
  234.3 4.3 copy-start.11
  247.4 4.7 copy-start.27
  250.1 1.9 copy-start.2
  255.8 5.2 copy-start.3
  255.8 5.2 copy-start.28
  264.1 2.1 copy-start.8
  266.2 1.3 copy-start.4
  266.2 1.9 copy-start.5
  267.1 3.0 copy-start.9
  267.1 1.3 copy-start.10
  268.6 4.3 copy-start.11
  274.9 15.9 %copy-start.23 = (s32[1,4,64]{2,1,0:T(4,128)S(1)}, s32[1,4,64]{2,1,0:T(4,128)}, u32[]{:S(2)}) copy-start(s32[1,4,64]{2,1,0:T(4,128)} %param.23) | copy-start | bytes 3076
  274.9 16.4 %copy-start.25 = (s32[1024]{0:T(1024)S(1)}, s32[1024]{0:T(1024)}, u32[]{:S(2)}) copy-start(s32[1024]{0:T(1024)} %copy-done.24) | copy-start | bytes 12292
  286.4 86.8 %all-to-all-start.1 = ((bf16[128,16,512]{2,1,0:T(8,128)(2,1)}), bf16[128,16,512]{2,1,0:T(8,128)(2,1)S(1)}, u32[]{:S(2)}, u32[]{:S(2)}) async-start(bf16[128,16,512]{2,1,0:T(8,128)(2,1)} %bitcast.193), calls=%async_computation.1 | async-start | bytes 4194304 | tf_op jit(solution)/shard_map/all_to_all | solution.py:254
  290.7 240.9 %all-reduce.8.cloned.1.call-start = ((), (), s32[]{:S(2)}) async-start(), calls=%async_computation.2 | async-start | bytes 5505024 | tf_op jit(solution)/shard_map/psum | solution.py:269
  373.2 4.5 copy-start.26
  377.1 2.6 copy-start.7
  500.3 18.1 %collective-permute-start.7 = (bf16[64,256]{1,0:T(8,128)(2,1)S(1)}, bf16[64,256]{1,0:T(8,128)(2,1)S(1)}, u32[]{:S(2)}, u32[]{:S(2)}) collective-permute-start(bf16[64,256]{1,0:T(8,128)(2,1)S(1)} %get-tuple-element.419), channel_id=1, source_target_pairs={{1,0},{2,1},{3,2},{4,3},{5,4},{6,5},{7,6},{8,7},{9,8},{10,9},{11,1... | collective-permute-start | bytes 98312 | tf_op jit(solution)/shard_map/ppermute | solution.py:19
  502.8 14.3 %collective-permute-start.6 = (bf16[64,256]{1,0:T(8,128)(2,1)S(1)}, bf16[64,256]{1,0:T(8,128)(2,1)S(1)}, u32[]{:S(2)}, u32[]{:S(2)}) collective-permute-start(bf16[64,256]{1,0:T(8,128)(2,1)S(1)} %get-tuple-element.420), channel_id=1, source_target_pairs={{0,1},{1,2},{2,3},{3,4},{4,5},{5,6},{6,7},{7,8},{8,9},{9,10},{10,1... | collective-permute-start | bytes 98312 | tf_op jit(solution)/shard_map/ppermute | solution.py:19
  506.2 9.6 %collective-permute-start.5 = (bf16[64,256]{1,0:T(8,128)(2,1)S(1)}, bf16[64,256]{1,0:T(8,128)(2,1)S(1)}, u32[]{:S(2)}, u32[]{:S(2)}) collective-permute-start(bf16[64,256]{1,0:T(8,128)(2,1)S(1)} %get-tuple-element.421), channel_id=1, source_target_pairs={{32,0},{64,32},{96,64},{33,1},{65,33},{97,65},{34,2},{66,34},{98,6... | collective-permute-start | bytes 98312 | tf_op jit(solution)/shard_map/ppermute | solution.py:19
  507.5 6.8 %collective-permute-start.4 = (bf16[64,256]{1,0:T(8,128)(2,1)S(1)}, bf16[64,256]{1,0:T(8,128)(2,1)S(1)}, u32[]{:S(2)}, u32[]{:S(2)}) collective-permute-start(bf16[64,256]{1,0:T(8,128)(2,1)S(1)} %get-tuple-element.422), channel_id=1, source_target_pairs={{0,32},{32,64},{64,96},{1,33},{33,65},{65,97},{2,34},{34,66},{66,9... | collective-permute-start | bytes 98312 | tf_op jit(solution)/shard_map/ppermute | solution.py:19
Sparse Core Ops, SparseCore 0:
  381.3 150.3 all-reduce.7
where the time goes:
time: 558 us; the launch traced here: 547 us
  other arithmetic  180 us (32%)
  local copies, waits for them, and re-layouts  133 us (24%)
  blocking collectives  81.3 us (15%)
  matrix products  51.8 us (9%)
  starting transfers between devices  48.9 us (9%)
  waiting for transfers between devices  34.8 us (6%)
  between operations  15.7 us (3%)
    scatter-add x16, other arithmetic, scatter_neighbour(): return total.at[near_tile[index]].add(spread)  105 us
    psum x1, blocking collectives, body(): lax.psum((near_grad, sums[0], sums[1], sums[2], sums[3], sums[4]), ('tx',...  81.3 us
    gather x16, local copies, waits for them, and re-layouts, add_neighbour(): jnp.take(extended, near_tile[index], axis=0).astype(jnp.float32)  63.1 us
    all_to_all x1, waiting for transfers between devices, body(): lax.all_to_all(outgoing, ('tx', 'ty'), split_axis=0, concat_axis=0, tiled...  23.7 us
    ppermute x8, starting transfers between devices, shifted(): lax.ppermute(value, axis, [(source, source + steps) for source in range(i...  22.5 us
    all_to_all x1, starting transfers between devices, body(): lax.all_to_all(outgoing, ('tx', 'ty'), split_axis=0, concat_axis=0, tiled...  22 us
    select_n x16, other arithmetic, add_neighbour(): jnp.take(extended, near_tile[index], axis=0).astype(jnp.float32)  12.4 us
    select_n x16, other arithmetic, scatter_neighbour(): return total.at[near_tile[index]].add(spread)  12.3 us
  transfers between devices with their start and end apart: 11, of which 2 were waited for; matrix products, arithmetic and copies ran while one was open for 29% of the time, Pallas kernels for 0%

commit v1 on v0

--- a/solution.py
+++ b/solution.py
@@ -36,22 +36,26 @@
     return lax.rsqrt(jnp.mean(value * value, axis=-1, keepdims=True) + eps_norm)
 
 
-def tile_forward(points_tile, halo_rows, near_tile, w_near):
+def near_counts(near_tile, ext_count):
+    rows = lax.broadcasted_iota(jnp.int32, (ext_count, near_tile.shape[1]), 0)
+    total = jnp.zeros((ext_count, near_tile.shape[1]), jnp.float32)
+    for index in range(near_tile.shape[0]):
+        total = total + (near_tile[index][None, :] == rows).astype(jnp.float32)
+    return total.astype(jnp.bfloat16)
+
+
+def tile_forward(points_tile, halo_rows, counts_t, w_near, count_near):
     extended = jnp.concatenate([points_tile, halo_rows], axis=0)
-    count_near = near_tile.shape[0]
-
-    def add_neighbour(index, total):
-        return total + jnp.take(extended, near_tile[index], axis=0).astype(jnp.float32)
-
-    total = lax.fori_loop(0, count_near, add_neighbour, jnp.zeros(points_tile.shape, jnp.float32))
+    total = lax.dot_general(
+        counts_t, extended, (((0,), (0,)), ((), ())), preferred_element_type=jnp.float32
+    )
     average = (total * (1.0 / count_near)).astype(jnp.bfloat16)
     linear_part = jnp.dot(average, w_near, preferred_element_type=jnp.float32)
     lifted = (points_tile.astype(jnp.float32) + gelu_tanh(linear_part)).astype(jnp.bfloat16)
     return (average, linear_part, lifted)
 
 
-def tile_backward(lifted_grad, average, linear_part, near_tile, w_near, ext_count):
-    count_near = near_tile.shape[0]
+def tile_backward(lifted_grad, average, linear_part, counts_t, w_near, count_near):
     tile_rows = lifted_grad.shape[0]
     act_grad = (lifted_grad.astype(jnp.float32) * gelu_slope(linear_part)).astype(jnp.bfloat16)
     near_grad = lax.dot_general(
@@ -60,12 +64,10 @@
     spread = lax.dot_general(
         act_grad, w_near, (((1,), (1,)), ((), ())), preferred_element_type=jnp.float32
     ) * (1.0 / count_near)
-
-    def scatter_neighbour(index, total):
-        return total.at[near_tile[index]].add(spread)
-
-    ext_grad = lax.fori_loop(
-        0, count_near, scatter_neighbour, jnp.zeros((ext_count, spread.shape[1]), jnp.float32)
+    spread_hi = spread.astype(jnp.bfloat16)
+    spread_lo = (spread - spread_hi.astype(jnp.float32)).astype(jnp.bfloat16)
+    ext_grad = jnp.dot(counts_t, spread_hi, preferred_element_type=jnp.float32) + jnp.dot(
+        counts_t, spread_lo, preferred_element_type=jnp.float32
     )
     row_grad = lifted_grad.astype(jnp.float32) + ext_grad[:tile_rows]
     halo_grad = ext_grad[tile_rows:].astype(jnp.bfloat16)
@@ -220,7 +222,9 @@
         ],
         axis=0,
     )
-    average, linear_part, lifted = tile_forward(points_tile, halo, near_tile, w_near)
+    count_near = near_tile.shape[0]
+    counts_t = near_counts(near_tile, tile_rows + 4 * border_rows)
+    average, linear_part, lifted = tile_forward(points_tile, halo, counts_t, w_near, count_near)
     rank, live = route_ranks(owner_tile, counts[0], tiles)
     slots = jnp.where(live, owner_tile * capacity + rank, tiles * capacity)
     payload = jnp.concatenate([lifted, grad_out[0]], axis=1)
@@ -255,8 +259,12 @@
     back_rows = jnp.take(returned, slots, axis=0, mode="fill", fill_value=0)
     out_rows = back_rows[:, :width]
     lifted_grad = back_rows[:, width:]
+    patch_flat = jnp.concatenate(
+        [sums[0], sums[2], sums[1].reshape(-1), sums[3].reshape(-1), sums[4].reshape(-1)]
+    )
+    patch_total = lax.psum(patch_flat, ("tx", "ty"))
     near_grad, row_grad, halo_grad = tile_backward(
-        lifted_grad, average, linear_part, near_tile, w_near, tile_rows + 4 * border_rows
+        lifted_grad, average, linear_part, counts_t, w_near, count_near
     )
     came_back = (
         pass_columns(halo_grad[0:border_rows], 1),
@@ -266,9 +274,14 @@
     )
     for direction in range(4):
         row_grad = row_grad.at[lists[direction]].add(came_back[direction].astype(jnp.float32))
-    near_sum, gain_one_sum, conv_sum, gain_two_sum, up_sum, down_sum = lax.psum(
-        (near_grad, sums[0], sums[1], sums[2], sums[3], sums[4]), ("tx", "ty")
-    )
+    near_sum = lax.psum(near_grad, ("tx", "ty"))
+    sizes = [width, width, conv_w.size, w_up.size, w_down.size]
+    shapes = [(width,), (width,), conv_w.shape, w_up.shape, w_down.shape]
+    offsets = [sum(sizes[:index]) for index in range(len(sizes))]
+    gain_one_sum, gain_two_sum, conv_sum, up_sum, down_sum = [
+        patch_total[start : start + size].reshape(shape)
+        for start, size, shape in zip(offsets, sizes, shapes)
+    ]
     totals = (gain_one_sum, conv_sum, gain_two_sum, up_sum, down_sum)
     scale = 1.0 / math.sqrt(tiles * tile_rows)
     return (

time: 558 us -> 418 us (0.75); the launches traced: 547 us -> 413 us
  waiting for transfers between devices: 34.8 us -> 170 us
  other arithmetic: 180 us -> 56.5 us
  blocking collectives: 81.3 us -> 0 us
  local copies, waits for them, and re-layouts: 133 us -> 75.2 us
  starting transfers between devices: 48.9 us -> 38.1 us
  matrix products: 51.8 us -> 57.5 us
    psum x1, waiting for transfers between devices: 11 us -> 126 us  [body(): near_sum = lax.psum(near_grad, ('tx', 'ty'))]
    scatter-add x16 -> x0, other arithmetic: 105 us -> none  [scatter_neighbour(): return total.at[near_tile[index]].add(spread)]
    psum x1 -> x0, blocking collectives: 81.3 us -> none  [body(): lax.psum((near_grad, sums[0], sums[1], sums[2], sums[3], sums[4]), ('tx',...]
    gather x16 -> x0, local copies, waits for them, and re-layouts: 63.1 us -> none  [add_neighbour(): jnp.take(extended, near_tile[index], axis=0).astype(jnp.float32)]
    select_n x32 -> x0, other arithmetic: 24.8 us -> none  [the longest x16 12.4 us: add_neighbour(): jnp.take(extended, near_tile[index], axis=0).astype(jnp.float32)]
    all_to_all x1, waiting for transfers between devices: 0.01 us -> 18.6 us  [body(): lax.all_to_all(back_slots, ('tx', 'ty'), split_axis=0, concat_axis=0, til...]
    convert_element_type x0 -> x1, other arithmetic: none -> 10.6 us  [near_counts(): return total.astype(jnp.bfloat16)]
    all_to_all x1, starting transfers between devices: 22 us -> 11.5 us  [body(): lax.all_to_all(outgoing, ('tx', 'ty'), split_axis=0, concat_axis=0, tiled...]
  transfers between devices with their start and end apart: 11 -> 11, of which waited for: 2 -> 3; matrix products, arithmetic and copies ran while one was open for 29% -> 12% of each run, Pallas kernels for 0% -> 0%
where the time goes in v1:
time: 418 us; the launch traced here: 413 us
  waiting for transfers between devices  170 us (41%)
  local copies, waits for them, and re-layouts  75.2 us (18%)
  matrix products  57.5 us (14%)
  other arithmetic  56.5 us (14%)
  starting transfers between devices  38.1 us (9%)
  between operations  15.7 us (4%)
    psum x1, waiting for transfers between devices, body(): near_sum = lax.psum(near_grad, ('tx', 'ty'))  126 us
    all_to_all x1, waiting for transfers between devices, body(): lax.all_to_all(outgoing, ('tx', 'ty'), split_axis=0, concat_axis=0, tiled...  24.7 us
    ppermute x8, starting transfers between devices, shifted(): lax.ppermute(value, axis, [(source, source + steps) for source in range(i...  22.2 us
    all_to_all x1, waiting for transfers between devices, body(): lax.all_to_all(back_slots, ('tx', 'ty'), split_axis=0, concat_axis=0, til...  18.6 us
    gather x2, local copies, waits for them, and re-layouts, body(): serial_both = jnp.take(incoming, zorder[0], axis=0)  12.2 us
    all_to_all x1, starting transfers between devices, body(): lax.all_to_all(outgoing, ('tx', 'ty'), split_axis=0, concat_axis=0, tiled...  11.5 us
    scatter x1, other arithmetic, body(): back_slots = jnp.zeros_like(back).at[zorder[0]].set(back)  11.5 us
    unnamed x57, local copies, waits for them, and re-layouts  11 us
  transfers between devices with their start and end apart: 11, of which 3 were waited for; matrix products, arithmetic and copies ran while one was open for 12% of the time, Pallas kernels for 0%

profile of v1, /device:TPU:1, one launch (start us, length us, event | category | flops | bytes accessed | tf_op | source)
XLA Modules:
  0.0 413.3 jit_solution(16206862345692908386)
XLA Ops:
  10.2 4.4 %sort.17 = (s32[1024]{0:T(1024)}, s32[1024]{0:T(1024)S(1)}) sort(s32[1024]{0:T(1024)S(1)} %add_select_fusion, s32[1024]{0:T(1024)S(1)} %iota.67), dimensions={0}, to_apply=%region_0.1 | sort | flops 10240 | bytes 16384 | tf_op jit(solution)/shard_map/jit(argsort)/sort | solution.py:82
  14.5 5.7 %gather_fusion = s32[1024]{0:T(1024)S(1)} fusion(s32[1024]{0:T(1024)} %bitcast.191, s32[1024]{0:T(1024)S(1)} %broadcast_clamp_fusion.3), kind=kCustom, calls=%fused_computation | custom fusion | bytes 12288 | tf_op jit(solution)/shard_map/jit(_take)/gather | solution.py:86
  21.6 4.6 %collective-permute-start.3 = (bf16[64,256]{1,0:T(8,128)(2,1)S(1)}, bf16[64,256]{1,0:T(8,128)(2,1)S(1)}, u32[]{:S(2)}, u32[]{:S(2)}) collective-permute-start(bf16[64,256]{1,0:T(8,128)(2,1)S(1)} %get-tuple-element.218), channel_id=1, source_target_pairs={{0,1},{1,2},{2,3},{3,4},{4,5},{5,6},{6,7},{7,8},{8,9},{9,10},{10,1... | collective-permute-start | bytes 98312 | tf_op jit(solution)/shard_map/ppermute | solution.py:19
  26.2 1.9 collective-permute-start.2
  28.1 3.5 collective-permute-start.1
  31.7 1.3 collective-permute-start
  33.8 6.6 %gather_fusion.1 = s32[1024]{0:T(1024)S(1)} fusion(s32[128]{0:T(128)S(1)} %sub.21, s32[1024]{0:T(1024)S(1)} %get-tuple-element.249), kind=kCustom, calls=%fused_computation.1 | custom fusion | bytes 12288 | tf_op jit(solution)/shard_map/jit(_take)/gather | solution.py:87
  40.5 4.8 %scatter_custom_fusion = s32[1024]{0:T(1024)S(1)} fusion(s32[1024]{0:T(1024)S(1)} %get-tuple-element.239, s32[1024]{0:T(1024)S(1)} %get-tuple-element.238, s32[]{:T(128)} %constant.71.clone.1), kind=kCustom, calls=%fused_computation.196 | custom fusion | bytes 4100 | tf_op jit(solution)/shard_map/scatter | solution.py:88
  45.2 10.6 %add_convert_fusion = bf16[1280,1024]{1,0:T(8,128)(2,1)S(1)} fusion(s32[1024]{0:T(1024)S(1)} %bitcast.230, s32[1024]{0:T(1024)S(1)} %bitcast.231, s32[1024]{0:T(1024)S(1)} %bitcast.217, s32[1024]{0:T(1024)S(1)} %bitcast.218, s32[1024]{0:T(1024)S(1)} %bitcast.219, s32[1024]{0:T(1024)S(1)} %bitcast.220, s32[1024]{0:T(1024)S(1)} %bitcast.221, ...), kind=kLoop, calls=%fused_computation.96 | loop fusion | flops 62914560 | bytes 2686976 | tf_op jit(solution)/shard_map/convert_element_type | solution.py:44
  57.6 1.5 add_convert_fusion.1
  59.1 6.7 %scatter_custom_fusion.1 = bf16[2048,512]{1,0:T(8,128)(2,1)} fusion(s32[1024]{0:T(1024)S(1)} %get-tuple-element.199, bf16[1024,256]{1,0:T(8,128)(2,1)S(1)} %bitcast.212, bf16[]{:T(256)} %constant.168, bf16[1024,256]{1,0:T(8,128)(2,1)S(1)} %get-tuple-element.244, bf16[]{:T(256)} %constant.86.clone.1), kind=kCustom, calls=%fused_computation.135 | custom fusion | flops 2097152 | bytes 3145732 | tf_op jit(solution)/shard_map/scatter | solution.py:232
  65.8 11.5 %all-to-all-start = ((bf16[128,16,512]{2,1,0:T(8,128)(2,1)}), bf16[128,16,512]{2,1,0:T(8,128)(2,1)S(1)}, u32[]{:S(2)}, u32[]{:S(2)}) async-start(bf16[128,16,512]{2,1,0:T(8,128)(2,1)} %bitcast.205), calls=%async_computation | async-start | bytes 4194304 | tf_op jit(solution)/shard_map/all_to_all | solution.py:234
  78.6 1.5 multiply_bitcast_fusion
  80.1 3.0 reshape.383
  83.2 24.7 %all-to-all-done = bf16[128,16,512]{2,1,0:T(8,128)(2,1)S(1)} async-done(((bf16[128,16,512]{2,1,0:T(8,128)(2,1)}), bf16[128,16,512]{2,1,0:T(8,128)(2,1)S(1)}, u32[]{:S(2)}, u32[]{:S(2)}) %all-to-all-start) | async-done | bytes 2097184 | tf_op jit(solution)/shard_map/all_to_all | solution.py:234
  107.8 9.2 %gather_fusion.3 = bf16[2048,512]{1,0:T(8,128)(2,1)} fusion(bf16[2048,512]{1,0:T(8,128)(2,1)S(1)} %bitcast.198, s32[2048]{0:T(1024)S(1)} %broadcast_clamp_fusion), kind=kCustom, calls=%fused_computation.3 | custom fusion | bytes 4202496 | tf_op jit(solution)/shard_map/jit(_take)/gather | solution.py:235
  117.1 3.0 copy.90
  120.1 1.6 broadcast_select_fusion
  121.6 68.8 %while.23 = (s32[]{:T(128)}, f32[256]{0:T(256)S(1)}, f32[3,8,32,32]{3,2,1,0:T(8,128)}, f32[256]{0:T(256)S(1)}, f32[256,1024]{1,0:T(8,128)}, /*index=5*/f32[1024,...) while((s32[]{:T(128)}, f32[256]{0:T(256)S(1)}, ...), condition=%wide.region_12.13_spmd.clone, body=%wide.region_5.12_spmd.clone.sunk | while | flops 4135946752 | bytes 123703776 | solution.py:251
  121.8 1.3 dynamic-slice_bitcast_fusion.2
  124.8 1.4 fusion.183
  127.4 1.3 multiply_reduce_fusion.2
  129.6 1.9 fusion.184
  131.4 2.0 copy-done.2
  133.4 2.5 fusion.192
  137.2 4.9 %convolution_add_fusion.12 = f32[1024,256]{1,0:T(8,128)} fusion(f32[1024,256]{1,0:T(8,128)} %get-tuple-element.385, pred[]{:T(512)S(6)} %compare.11, bf16[1024,512]{0,1:T(8,128)(2,1)S(1)} %dynamic-slice_bitcast_fusion.2, f32[1024,1024]{1,0:T(8,128)} %copy-done.2), kind=kOutput, calls=%fused_computation.34.clone.1 | convolution fusion | flops 546832384 | bytes 6815745 | tf_op jit(solution)/shard_map/while/body/eval_jaxpr/dot_general | solution.py:137
  142.1 3.0 fusion.185
  145.2 2.1 fusion.186
  149.7 1.5 fusion.189
  152.4 1.5 fusion.190
  155.9 1.3 dynamic-slice_bitcast_fusion.2
  158.8 1.4 fusion.183
  161.5 1.3 multiply_reduce_fusion.2
  163.6 1.9 fusion.184
  165.5 2.0 copy-done.2
  167.5 2.5 fusion.192
  171.3 5.2 %convolution_add_fusion.12 = f32[1024,256]{1,0:T(8,128)} fusion(f32[1024,256]{1,0:T(8,128)} %get-tuple-element.385, pred[]{:T(512)S(6)} %compare.11, bf16[1024,512]{0,1:T(8,128)(2,1)S(1)} %dynamic-slice_bitcast_fusion.2, f32[1024,1024]{1,0:T(8,128)} %copy-done.2), kind=kOutput, calls=%fused_computation.34.clone.1 | convolution fusion | flops 546832384 | bytes 6815745 | tf_op jit(solution)/shard_map/while/body/eval_jaxpr/dot_general | solution.py:137
  176.5 3.0 fusion.185
  179.6 2.1 fusion.186
  184.1 1.5 fusion.189
  186.8 1.5 fusion.190
  190.5 11.5 %scatter_custom_fusion.2 = bf16[2048,512]{1,0:T(8,128)(2,1)} fusion(s32[2048]{0:T(1024)} %bitcast.215, bf16[2048,256]{1,0:T(8,128)(2,1)} %bitcast.209, bf16[]{:T(256)} %constant.168, bf16[2048,256]{1,0:T(8,128)(2,1)} %bitcast.210, bf16[]{:T(256)} %constant.86.clone.1), kind=kCustom, calls=%fused_computation.114 | custom fusion | flops 4194304 | bytes 4195328 | tf_op jit(solution)/shard_map/scatter | solution.py:257
  202.0 4.4 %all-to-all-start.1 = ((bf16[128,16,512]{2,1,0:T(8,128)(2,1)}), bf16[128,16,512]{2,1,0:T(8,128)(2,1)S(1)}, u32[]{:S(2)}, u32[]{:S(2)}) async-start(bf16[128,16,512]{2,1,0:T(8,128)(2,1)} %bitcast.204), calls=%async_computation.1 | async-start | bytes 4194304 | tf_op jit(solution)/shard_map/all_to_all | solution.py:258
  207.9 1.8 copy.105
  212.2 1.5 constant_dynamic-update-slice_fusion.10
  213.7 2.4 constant_dynamic-update-slice_fusion.9
  216.1 2.4 constant_dynamic-update-slice_fusion.8
  218.5 18.6 %all-to-all-done.1 = bf16[128,16,512]{2,1,0:T(8,128)(2,1)S(1)} async-done(((bf16[128,16,512]{2,1,0:T(8,128)(2,1)}), bf16[128,16,512]{2,1,0:T(8,128)(2,1)S(1)}, u32[]{:S(2)}, u32[]{:S(2)}) %all-to-all-start.1) | async-done | bytes 2097184 | tf_op jit(solution)/shard_map/all_to_all | solution.py:258
  237.1 5.1 %gather_fusion.4 = bf16[1024,512]{1,0:T(8,128)(2,1)} fusion(bf16[2048,512]{1,0:T(8,128)(2,1)S(1)} %bitcast.199, s32[1024]{0:T(1024)S(1)} %broadcast_clamp_fusion.1), kind=kCustom, calls=%fused_computation.4 | custom fusion | bytes 2101248 | tf_op jit(solution)/shard_map/jit(_take)/gather | solution.py:259
  242.1 1.6 broadcast_select_fusion.1
  244.7 1.9 fusion.58
  249.0 2.0 fusion.72
  251.0 2.9 fusion.93
  253.9 2.8 collective-permute-start.7
  256.7 2.7 collective-permute-start.6
  259.5 1.3 collective-permute-start.5
  260.8 4.0 collective-permute-start.4
  265.8 1.3 scatter_custom_fusion.3
  267.1 1.3 scatter_custom_fusion.4
  268.5 1.3 scatter_custom_fusion.5
  269.9 1.3 scatter_custom_fusion.6
  272.1 126.2 %all-reduce.7.cloned.1.call-done = (f32[256,256]{1,0:T(8,128)}, f32[549376]{0:T(1024)}) async-done(((f32[256,256]{1,0:T(8,128)}, f32[549376]{0:T(1024)}), (f32[256,256]{1,0:T(8,128)}, f32[549376]{0:T(1024)})) %all-reduce.7.cloned.1.call-update) | async-done | bytes 2459664 | tf_op jit(solution)/shard_map/psum | solution.py:277
  398.2 1.3 slice_multiply_fusion.3
  400.5 1.8 slice_multiply_fusion
  (196 shorter events, 42.4 us)
Async XLA Ops:
  7.2 50.4 %copy-start = (bf16[256,256]{1,0:T(8,128)(2,1)S(1)}, bf16[256,256]{1,0:T(8,128)(2,1)}, u32[]{:S(2)}) copy-start(bf16[256,256]{1,0:T(8,128)(2,1)} %param.21) | copy-start | bytes 393220
  7.2 25.8 %copy-start.1 = (s32[1,1024]{1,0:T(1,128)S(1)}, s32[1,1024]{1,0:T(1,128)}, u32[]{:S(2)}) copy-start(s32[1,1024]{1,0:T(1,128)} %param.17) | copy-start | bytes 12292
  7.2 13.1 %copy-start.16 = (bf16[1,1024,256]{2,1,0:T(8,128)(2,1)S(1)}, bf16[1,1024,256]{2,1,0:T(8,128)(2,1)}, u32[]{:S(2)}) copy-start(bf16[1,1024,256]{2,1,0:T(8,128)(2,1)} %param.15) | copy-start | bytes 1572868
  20.3 20.1 %copy-start.24 = (s32[1,16,1024]{2,1,0:T(8,128)S(1)}, s32[1,16,1024]{2,1,0:T(8,128)}, u32[]{:S(2)}) copy-start(s32[1,16,1024]{2,1,0:T(8,128)} %param.20) | copy-start | bytes 196612
  21.6 35.0 %collective-permute-start.3 = (bf16[64,256]{1,0:T(8,128)(2,1)S(1)}, bf16[64,256]{1,0:T(8,128)(2,1)S(1)}, u32[]{:S(2)}, u32[]{:S(2)}) collective-permute-start(bf16[64,256]{1,0:T(8,128)(2,1)S(1)} %get-tuple-element.218), channel_id=1, source_target_pairs={{0,1},{1,2},{2,3},{3,4},{4,5},{5,6},{6,7},{7,8},{8,9},{9,10},{10,1... | collective-permute-start | bytes 98312 | tf_op jit(solution)/shard_map/ppermute | solution.py:19
  26.2 30.4 %collective-permute-start.2 = (bf16[64,256]{1,0:T(8,128)(2,1)S(1)}, bf16[64,256]{1,0:T(8,128)(2,1)S(1)}, u32[]{:S(2)}, u32[]{:S(2)}) collective-permute-start(bf16[64,256]{1,0:T(8,128)(2,1)S(1)} %get-tuple-element.219), channel_id=1, source_target_pairs={{1,0},{2,1},{3,2},{4,3},{5,4},{6,5},{7,6},{8,7},{9,8},{10,9},{11,1... | collective-permute-start | bytes 98312 | tf_op jit(solution)/shard_map/ppermute | solution.py:19
  28.1 28.4 %collective-permute-start.1 = (bf16[64,256]{1,0:T(8,128)(2,1)S(1)}, bf16[64,256]{1,0:T(8,128)(2,1)S(1)}, u32[]{:S(2)}, u32[]{:S(2)}) collective-permute-start(bf16[64,256]{1,0:T(8,128)(2,1)S(1)} %get-tuple-element.220), channel_id=1, source_target_pairs={{0,32},{32,64},{64,96},{1,33},{33,65},{65,97},{2,34},{34,66},{66,9... | collective-permute-start | bytes 98312 | tf_op jit(solution)/shard_map/ppermute | solution.py:19
  31.7 24.8 %collective-permute-start = (bf16[64,256]{1,0:T(8,128)(2,1)S(1)}, bf16[64,256]{1,0:T(8,128)(2,1)S(1)}, u32[]{:S(2)}, u32[]{:S(2)}) collective-permute-start(bf16[64,256]{1,0:T(8,128)(2,1)S(1)} %get-tuple-element.221), channel_id=1, source_target_pairs={{32,0},{64,32},{96,64},{33,1},{65,33},{97,65},{34,2},{66,34},{98,6... | collective-permute-start | bytes 98312 | tf_op jit(solution)/shard_map/ppermute | solution.py:19
  55.9 3.1 copy-start.6
  56.5 2.5 copy-start.28
  56.6 2.5 copy-start.19
  57.5 1.5 copy-start.17
  59.0 18.9 %copy-start.25 = (s32[1,2048]{1,0:T(1,128)S(1)}, s32[1,2048]{1,0:T(1,128)}, u32[]{:S(2)}) copy-start(s32[1,2048]{1,0:T(1,128)} %param.18) | copy-start | bytes 24580
  59.0 19.6 %copy-start.23 = (bf16[3,8,32,32]{3,2,1,0:T(8,128)(2,1)S(1)}, bf16[3,8,32,32]{3,2,1,0:T(8,128)(2,1)}, u32[]{:S(2)}) copy-start(bf16[3,8,32,32]{3,2,1,0:T(8,128)(2,1)} %param.23) | copy-start | bytes 147460
  65.8 42.1 %all-to-all-start = ((bf16[128,16,512]{2,1,0:T(8,128)(2,1)}), bf16[128,16,512]{2,1,0:T(8,128)(2,1)S(1)}, u32[]{:S(2)}, u32[]{:S(2)}) async-start(bf16[128,16,512]{2,1,0:T(8,128)(2,1)} %bitcast.205), calls=%async_computation | async-start | bytes 4194304 | tf_op jit(solution)/shard_map/all_to_all | solution.py:234
  83.1 33.9 %copy-start.26 = (s32[2048,1]{0,1:T(1,128)}, s32[2048,1]{0,1:T(1,128)S(1)}, u32[]{:S(2)}) copy-start(s32[2048,1]{0,1:T(1,128)S(1)} %compare_select_fusion) | copy-start | bytes 24580
  117.0 4.6 %copy-start.20 = (f32[256]{0:T(256)S(1)}, f32[256]{0:T(256)}, u32[]{:S(2)}) copy-start(f32[256]{0:T(256)} %param.24) | copy-start | bytes 3076
  117.0 4.6 %copy-start.22 = (f32[256]{0:T(256)S(1)}, f32[256]{0:T(256)}, u32[]{:S(2)}) copy-start(f32[256]{0:T(256)} %param.22) | copy-start | bytes 3076
  128.7 4.7 %copy-start.31 = (bf16[1024,256]{1,0:T(8,128)(2,1)S(1)}, bf16[1024,256]{1,0:T(8,128)(2,1)}, u32[]{:S(2)}) copy-start(bf16[1024,256]{1,0:T(8,128)(2,1)} %get-tuple-element.408) | copy-start | bytes 1572868 | tf_op jit(solution)/shard_map/while
  131.4 2.0 copy-start.2
  137.2 4.9 %copy-start.3 = (f32[1024,1024]{1,0:T(8,128)S(1)}, f32[1024,1024]{1,0:T(8,128)}, u32[]{:S(2)}) copy-start(f32[1024,1024]{1,0:T(8,128)} %copy-done.2) | copy-start | bytes 12582916 | tf_op jit(solution)/shard_map/while
  137.2 4.9 %copy-start.32 = (bf16[1024,256]{1,0:T(8,128)(2,1)S(1)}, bf16[1024,256]{1,0:T(8,128)(2,1)}, u32[]{:S(2)}) copy-start(bf16[1024,256]{1,0:T(8,128)(2,1)} %get-tuple-element.408) | copy-start | bytes 1572868 | tf_op jit(solution)/shard_map/while
  145.2 2.1 copy-start.8
  147.3 1.3 copy-start.4
  147.3 1.9 copy-start.5
  148.2 3.0 copy-start.9
  148.2 1.3 copy-start.11
  149.7 4.3 %copy-start.12 = (f32[3,8,32,32]{3,2,1,0:T(8,128)}, f32[3,8,32,32]{3,2,1,0:T(8,128)S(1)}, u32[]{:S(2)}) copy-start(f32[3,8,32,32]{3,2,1,0:T(8,128)S(1)} %maximum_add_fusion.2) | copy-start | bytes 294916 | tf_op jit(solution)/shard_map/while
  162.8 4.7 %copy-start.31 = (bf16[1024,256]{1,0:T(8,128)(2,1)S(1)}, bf16[1024,256]{1,0:T(8,128)(2,1)}, u32[]{:S(2)}) copy-start(bf16[1024,256]{1,0:T(8,128)(2,1)} %get-tuple-element.408) | copy-start | bytes 1572868 | tf_op jit(solution)/shard_map/while
  165.5 2.0 copy-start.2
  171.3 5.2 %copy-start.3 = (f32[1024,1024]{1,0:T(8,128)S(1)}, f32[1024,1024]{1,0:T(8,128)}, u32[]{:S(2)}) copy-start(f32[1024,1024]{1,0:T(8,128)} %copy-done.2) | copy-start | bytes 12582916 | tf_op jit(solution)/shard_map/while
  171.3 5.2 %copy-start.32 = (bf16[1024,256]{1,0:T(8,128)(2,1)S(1)}, bf16[1024,256]{1,0:T(8,128)(2,1)}, u32[]{:S(2)}) copy-start(bf16[1024,256]{1,0:T(8,128)(2,1)} %get-tuple-element.408) | copy-start | bytes 1572868 | tf_op jit(solution)/shard_map/while
  179.5 2.1 copy-start.8
  181.7 1.3 copy-start.4
  181.7 1.9 copy-start.5
  182.6 3.0 copy-start.9
  182.6 1.3 copy-start.11
  184.1 4.3 %copy-start.12 = (f32[3,8,32,32]{3,2,1,0:T(8,128)}, f32[3,8,32,32]{3,2,1,0:T(8,128)S(1)}, u32[]{:S(2)}) copy-start(f32[3,8,32,32]{3,2,1,0:T(8,128)S(1)} %maximum_add_fusion.2) | copy-start | bytes 294916 | tf_op jit(solution)/shard_map/while
  190.5 16.0 %copy-start.27 = (s32[1,4,64]{2,1,0:T(4,128)S(1)}, s32[1,4,64]{2,1,0:T(4,128)}, u32[]{:S(2)}) copy-start(s32[1,4,64]{2,1,0:T(4,128)} %param.19) | copy-start | bytes 3076
  190.5 16.0 %copy-start.29 = (s32[1024]{0:T(1024)S(1)}, s32[1024]{0:T(1024)}, u32[]{:S(2)}) copy-start(s32[1024]{0:T(1024)} %copy-done.28) | copy-start | bytes 12292
  190.5 17.1 %copy-start.10 = (f32[256,1024]{1,0:T(8,128)S(1)}, f32[256,1024]{1,0:T(8,128)}, u32[]{:S(2)}) copy-start(f32[256,1024]{1,0:T(8,128)} %get-tuple-element.93) | copy-start | bytes 3145732
  202.0 35.0 %all-to-all-start.1 = ((bf16[128,16,512]{2,1,0:T(8,128)(2,1)}), bf16[128,16,512]{2,1,0:T(8,128)(2,1)S(1)}, u32[]{:S(2)}, u32[]{:S(2)}) async-start(bf16[128,16,512]{2,1,0:T(8,128)(2,1)} %bitcast.204), calls=%async_computation.1 | async-start | bytes 4194304 | tf_op jit(solution)/shard_map/all_to_all | solution.py:258
  206.4 191.9 %all-reduce.7.cloned.1.call-start = ((), (), s32[]{:S(2)}) async-start(), calls=%async_computation.2 | async-start | bytes 4923392 | tf_op jit(solution)/shard_map/psum | solution.py:277
  237.0 5.1 %copy-start.30 = (pred[1024]{0:T(1024)(128)(4,1)S(1)}, pred[1024]{0:T(1024)(128)(4,1)}, u32[]{:S(2)}) copy-start(pred[1024]{0:T(1024)(128)(4,1)} %get-tuple-element.198) | copy-start | bytes 3076
  242.1 4.5 %copy-start.18 = (bf16[1024,256]{1,0:T(8,128)(2,1)S(1)}, bf16[1024,256]{1,0:T(8,128)(2,1)}, u32[]{:S(2)}) copy-start(bf16[1024,256]{1,0:T(8,128)(2,1)} %copy-done.17) | copy-start | bytes 1572868
  242.1 6.9 %copy-start.7 = (bf16[1280,1024]{1,0:T(8,128)(2,1)S(1)}, bf16[1280,1024]{1,0:T(8,128)(2,1)}, u32[]{:S(2)}) copy-start(bf16[1280,1024]{1,0:T(8,128)(2,1)} %copy-done.6) | copy-start | bytes 7864324
  243.7 1.0 copy-start.14
  248.0 1.0 copy-start.13
  251.0 13.8 %copy-start.15 = (bf16[1024,512]{1,0:T(8,128)(2,1)S(1)}, bf16[1024,512]{1,0:T(8,128)(2,1)}, u32[]{:S(2)}) copy-start(bf16[1024,512]{1,0:T(8,128)(2,1)} %copy-done.14) | copy-start | bytes 3145732
  253.9 16.0 %collective-permute-start.7 = (bf16[64,256]{1,0:T(8,128)(2,1)S(1)}, bf16[64,256]{1,0:T(8,128)(2,1)S(1)}, u32[]{:S(2)}, u32[]{:S(2)}) collective-permute-start(bf16[64,256]{1,0:T(8,128)(2,1)S(1)} %get-tuple-element.214), channel_id=1, source_target_pairs={{1,0},{2,1},{3,2},{4,3},{5,4},{6,5},{7,6},{8,7},{9,8},{10,9},{11,1... | collective-permute-start | bytes 98312 | tf_op jit(solution)/shard_map/ppermute | solution.py:19
  256.7 11.8 %collective-permute-start.6 = (bf16[64,256]{1,0:T(8,128)(2,1)S(1)}, bf16[64,256]{1,0:T(8,128)(2,1)S(1)}, u32[]{:S(2)}, u32[]{:S(2)}) collective-permute-start(bf16[64,256]{1,0:T(8,128)(2,1)S(1)} %get-tuple-element.215), channel_id=1, source_target_pairs={{0,1},{1,2},{2,3},{3,4},{4,5},{5,6},{6,7},{7,8},{8,9},{9,10},{10,1... | collective-permute-start | bytes 98312 | tf_op jit(solution)/shard_map/ppermute | solution.py:19
  259.5 7.6 %collective-permute-start.5 = (bf16[64,256]{1,0:T(8,128)(2,1)S(1)}, bf16[64,256]{1,0:T(8,128)(2,1)S(1)}, u32[]{:S(2)}, u32[]{:S(2)}) collective-permute-start(bf16[64,256]{1,0:T(8,128)(2,1)S(1)} %get-tuple-element.216), channel_id=1, source_target_pairs={{32,0},{64,32},{96,64},{33,1},{65,33},{97,65},{34,2},{66,34},{98,6... | collective-permute-start | bytes 98312 | tf_op jit(solution)/shard_map/ppermute | solution.py:19
  260.8 5.0 %collective-permute-start.4 = (bf16[64,256]{1,0:T(8,128)(2,1)S(1)}, bf16[64,256]{1,0:T(8,128)(2,1)S(1)}, u32[]{:S(2)}, u32[]{:S(2)}) collective-permute-start(bf16[64,256]{1,0:T(8,128)(2,1)S(1)} %get-tuple-element.217), channel_id=1, source_target_pairs={{0,32},{32,64},{64,96},{1,33},{33,65},{65,97},{2,34},{34,66},{66,9... | collective-permute-start | bytes 98312 | tf_op jit(solution)/shard_map/ppermute | solution.py:19
  398.2 4.0 copy-start.21
Sparse Core Ops, SparseCore 0:
  251.1 147.1 all-reduce.6

commit v2 on v1

--- a/solution.py
+++ b/solution.py
@@ -90,11 +90,15 @@
 
 
 def shift_down(rows):
-    return jnp.concatenate([jnp.zeros_like(rows[:1]), rows[:-1]], axis=0)
+    patches = rows.reshape(-1, PATCH, rows.shape[-1])
+    moved = jnp.concatenate([jnp.zeros_like(patches[:, :1]), patches[:, :-1]], axis=1)
+    return moved.reshape(rows.shape)
 
 
 def shift_up(rows):
-    return jnp.concatenate([rows[1:], jnp.zeros_like(rows[:1])], axis=0)
+    patches = rows.reshape(-1, PATCH, rows.shape[-1])
+    moved = jnp.concatenate([patches[:, 1:], jnp.zeros_like(patches[:, :1])], axis=1)
+    return moved.reshape(rows.shape)
 
 
 def block_taps(conv_w):
@@ -234,22 +238,9 @@
     incoming = lax.all_to_all(outgoing, ("tx", "ty"), split_axis=0, concat_axis=0, tiled=True)
     serial_both = jnp.take(incoming, zorder[0], axis=0)
     taps_full = block_taps(conv_w)
-    zero_sums = (
-        jnp.zeros((width,), jnp.float32),
-        jnp.zeros(conv_w.shape, jnp.float32),
-        jnp.zeros((width,), jnp.float32),
-        jnp.zeros(w_up.shape, jnp.float32),
-        jnp.zeros(w_down.shape, jnp.float32),
-    )
-
-    def patch_step(carry, block):
-        result, serial_grad, grads = patch_pass(
-            block[:, :width], block[:, width:], gain_one, conv_w, taps_full, gain_two, w_up, w_down
-        )
-        return (jax.tree.map(lambda left, right: left + right, carry, grads), (result, serial_grad))
-
-    sums, (results, serial_grads) = lax.scan(
-        patch_step, zero_sums, serial_both.reshape(recv_rows // PATCH, PATCH, 2 * width)
+
+    results, serial_grads, sums = patch_pass(
+        serial_both[:, :width], serial_both[:, width:], gain_one, conv_w, taps_full, gain_two, w_up, w_down
     )
     back = jnp.concatenate(
         [results.reshape(recv_rows, width), serial_grads.reshape(recv_rows, width)], axis=1
@@ -274,6 +265,7 @@
     )
     for direction in range(4):
         row_grad = row_grad.at[lists[direction]].add(came_back[direction].astype(jnp.float32))
+    row_grad, near_grad, patch_total = lax.optimization_barrier((row_grad, near_grad, patch_total))
     near_sum = lax.psum(near_grad, ("tx", "ty"))
     sizes = [width, width, conv_w.size, w_up.size, w_down.size]
     shapes = [(width,), (width,), conv_w.shape, w_up.shape, w_down.shape]

time: 418 us -> 543 us (1.30)
  waiting for transfers between devices: 170 us -> 281 us
  local copies, waits for them, and re-layouts: 75.2 us -> 102 us
  matrix products: 57.5 us -> 43.2 us
    psum x0 -> x1, waiting for transfers between devices: none -> 107 us  [body(): patch_total = lax.psum(patch_flat, ('tx', 'ty'))]
    psum x1, waiting for transfers between devices: 126 us -> 139 us  [body(): near_sum = lax.psum(near_grad, ('tx', 'ty'))]
    scatter x1 -> x0, other arithmetic: 11.5 us -> none  [body(): back_slots = jnp.zeros_like(back).at[zorder[0]].set(back)]
    scatter x0 -> x1, local copies, waits for them, and re-layouts: none -> 11.5 us  [body(): back_slots = jnp.zeros_like(back).at[zorder[0]].set(back)]
    scatter-add x4, other arithmetic: 5.37 us -> 12.7 us  [body(): row_grad.at[lists[direction]].add(came_back[direction].astype(jnp.float32))]
    all_to_all x1, waiting for transfers between devices: 18.6 us -> 12.3 us  [body(): lax.all_to_all(back_slots, ('tx', 'ty'), split_axis=0, concat_axis=0, til...]
    unnamed x57 -> x90, local copies, waits for them, and re-layouts: 11 us -> 11.4 us
  transfers between devices with their start and end apart: 11 -> 12, of which waited for: 3 -> 4; matrix products, arithmetic and copies ran while one was open for 12% -> 14% of each run, Pallas kernels for 0% -> 0%
where the time goes in v2:
time: 543 us; the launch traced here: 533 us
  waiting for transfers between devices  281 us (52%)
  local copies, waits for them, and re-layouts  102 us (19%)
  other arithmetic  55.1 us (10%)
  matrix products  43.2 us (8%)
  starting transfers between devices  36 us (7%)
  between operations  15.8 us (3%)
    psum x1, waiting for transfers between devices, body(): near_sum = lax.psum(near_grad, ('tx', 'ty'))  139 us
    psum x1, waiting for transfers between devices, body(): patch_total = lax.psum(patch_flat, ('tx', 'ty'))  107 us
    all_to_all x1, waiting for transfers between devices, body(): lax.all_to_all(outgoing, ('tx', 'ty'), split_axis=0, concat_axis=0, tiled...  22.8 us
    ppermute x8, starting transfers between devices, shifted(): lax.ppermute(value, axis, [(source, source + steps) for source in range(i...  20.4 us
    gather x2, local copies, waits for them, and re-layouts, body(): serial_both = jnp.take(incoming, zorder[0], axis=0)  13.1 us
    scatter-add x4, other arithmetic, body(): row_grad.at[lists[direction]].add(came_back[direction].astype(jnp.float32))  12.7 us
    all_to_all x1, waiting for transfers between devices, body(): lax.all_to_all(back_slots, ('tx', 'ty'), split_axis=0, concat_axis=0, til...  12.3 us
    scatter x1, local copies, waits for them, and re-layouts, body(): back_slots = jnp.zeros_like(back).at[zorder[0]].set(back)  11.5 us
  transfers between devices with their start and end apart: 12, of which 4 were waited for; matrix products, arithmetic and copies ran while one was open for 14% of the time, Pallas kernels for 0%

profile of v2, /device:TPU:1, one launch (start us, length us, event | category | flops | bytes accessed | tf_op | source)
XLA Modules:
  0.0 533.1 jit_solution(16888555418986480388)
XLA Ops:
  10.1 4.4 sort.17
  14.5 4.5 gather_fusion
  21.7 5.0 collective-permute-start.1
  26.7 2.9 collective-permute-start.2
  29.6 3.2 collective-permute-start.3
  33.7 6.6 %gather_fusion.1 = s32[1024]{0:T(1024)S(1)} fusion(s32[128]{0:T(128)S(1)} %sub.21, s32[1024]{0:T(1024)S(1)} %get-tuple-element.94), kind=kCustom, calls=%fused_computation.1 | custom fusion | bytes 12288 | tf_op jit(solution)/shard_map/jit(_take)/gather | solution.py:87
  40.3 4.3 scatter_custom_fusion
  44.6 10.6 %add_convert_fusion = bf16[1280,1024]{1,0:T(8,128)(2,1)S(1)} fusion(s32[1024]{0:T(1024)S(1)} %bitcast.175, s32[1024]{0:T(1024)S(1)} %bitcast.176, s32[1024]{0:T(1024)S(1)} %bitcast.162, s32[1024]{0:T(1024)S(1)} %bitcast.163, s32[1024]{0:T(1024)S(1)} %bitcast.164, s32[1024]{0:T(1024)S(1)} %bitcast.165, s32[1024]{0:T(1024)S(1)} %bitcast.166, ...), kind=kLoop, calls=%fused_computation.22 | loop fusion | flops 62914560 | bytes 2686976 | tf_op jit(solution)/shard_map/convert_element_type | solution.py:44
  57.0 1.5 add_convert_fusion.1
  58.5 6.8 %scatter_custom_fusion.1 = bf16[2048,512]{1,0:T(8,128)(2,1)} fusion(s32[1024]{0:T(1024)S(1)} %get-tuple-element.45, bf16[1024,256]{1,0:T(8,128)(2,1)S(1)} %bitcast.156, bf16[]{:T(256)} %constant.144, bf16[1024,256]{1,0:T(8,128)(2,1)S(1)} %get-tuple-element.85, bf16[]{:T(256)} %constant.59.clone.1), kind=kCustom, calls=%fused_computation.99 | custom fusion | flops 2097152 | bytes 3145732 | tf_op jit(solution)/shard_map/scatter | solution.py:236
  65.3 11.2 %all-to-all-start = ((bf16[128,16,512]{2,1,0:T(8,128)(2,1)}), bf16[128,16,512]{2,1,0:T(8,128)(2,1)S(1)}, u32[]{:S(2)}, u32[]{:S(2)}) async-start(bf16[128,16,512]{2,1,0:T(8,128)(2,1)} %bitcast.148), calls=%async_computation | async-start | bytes 4194304 | tf_op jit(solution)/shard_map/all_to_all | solution.py:238
  77.9 2.1 squeeze.54
  80.0 1.4 reshape.499
  82.1 1.4 squeeze.55
  84.2 22.8 %all-to-all-done = bf16[128,16,512]{2,1,0:T(8,128)(2,1)S(1)} async-done(((bf16[128,16,512]{2,1,0:T(8,128)(2,1)}), bf16[128,16,512]{2,1,0:T(8,128)(2,1)S(1)}, u32[]{:S(2)}, u32[]{:S(2)}) %all-to-all-start) | async-done | bytes 2097184 | tf_op jit(solution)/shard_map/all_to_all | solution.py:238
  107.0 9.2 %gather_fusion.3 = bf16[2048,512]{1,0:T(8,128)(2,1)} fusion(bf16[2048,512]{1,0:T(8,128)(2,1)S(1)} %bitcast.137, s32[2048]{0:T(1024)S(1)} %broadcast_clamp_fusion), kind=kCustom, calls=%fused_computation.3 | custom fusion | bytes 4202496 | tf_op jit(solution)/shard_map/jit(_take)/gather | solution.py:239
  116.2 4.0 copy.84
  120.2 1.8 broadcast_select_fusion
  122.3 1.4 fusion.24
  123.6 2.6 reshape.388
  126.3 4.1 fusion.70
  130.3 1.6 concatenate.26
  136.0 1.4 fusion.67
  137.5 6.5 %fusion.6 = bf16[2048,1024]{1,0:T(8,128)(2,1)S(1)} fusion(f32[2048,1024]{1,0:T(8,128)S(1)} %fusion.67, bf16[1024,256]{1,0:T(8,128)(2,1)S(1)} %copy-done.37, bf16[2048,512]{0,1:T(8,128)(2,1)S(1)} %broadcast_select_fusion), kind=kOutput, calls=%fused_computation.20 | convolution fusion | flops 1117782016 | bytes 14155776 | tf_op jit(solution)/shard_map/dot_general | solution.py:144
  144.0 2.3 convolution_bitcast_fusion.1
  146.2 2.6 fusion.23
  148.9 2.7 reshape_reshape.7
  151.6 2.6 reshape_reshape.6
  154.2 7.7 %fusion.13 = bf16[2048,256]{0,1:T(8,128)(2,1)} fusion(f32[2048,256]{0,1:T(8,128)} %copy-done.6, bf16[1024,256]{1,0:T(8,128)(2,1)S(1)} %copy-done.38, f32[2048,1024]{1,0:T(8,128)} %copy-done.12), kind=kOutput, calls=%fused_computation.56 | convolution fusion | flops 1093664768 | bytes 12058624 | tf_op jit(solution)/shard_map/dot_general | solution.py:138
  163.9 1.7 fusion.68
  165.7 2.3 copy.95
  167.9 1.7 fusion.37
  169.6 1.5 concatenate.28
  171.1 2.9 copy.93
  174.0 1.7 fusion.35
  175.7 1.5 concatenate.29
  177.2 2.9 copy.94
  180.1 3.6 fusion.26
  183.8 1.3 fusion.19
  185.4 2.7 copy.89
  188.1 11.5 %scatter_custom_fusion.2 = bf16[2048,512]{1,0:T(8,128)(2,1)} fusion(s32[2048]{0:T(1024)S(1)} %bitcast.160, bf16[2048,512]{1,0:T(8,128)(2,1)} %copy.89, bf16[]{:T(256)} %constant.59.clone.1), kind=kCustom, calls=%fused_computation.107 | custom fusion | bytes 2097664 | tf_op jit(solution)/shard_map/scatter | solution.py:248
  199.5 4.4 all-to-all-start.1
  204.0 2.1 convolution_bitcast_fusion.2
  207.1 5.6 %convolution_bitcast_fusion = f32[128,2,8,128]{3,2,1,0:T(8,128)S(1)} fusion(bf16[2048,512]{0,1:T(8,128)(2,1)} %copy-done.5, f32[2048,1024]{1,0:T(8,128)} %copy-done.12), kind=kOutput, calls=%fused_computation.79 | convolution fusion | flops 1092616192 | bytes 10485760 | tf_op jit(solution)/shard_map/dot_general | solution.py:141
  213.3 1.3 constant_dynamic-update-slice_fusion.5
  215.9 1.5 constant_dynamic-update-slice_fusion.8
  217.4 2.3 constant_dynamic-update-slice_fusion.7
  219.8 2.4 constant_dynamic-update-slice_fusion.6
  222.3 12.3 %all-to-all-done.1 = bf16[128,16,512]{2,1,0:T(8,128)(2,1)S(1)} async-done(((bf16[128,16,512]{2,1,0:T(8,128)(2,1)}), bf16[128,16,512]{2,1,0:T(8,128)(2,1)S(1)}, u32[]{:S(2)}, u32[]{:S(2)}) %all-to-all-start.1) | async-done | bytes 2097184 | tf_op jit(solution)/shard_map/all_to_all | solution.py:249
  234.6 5.1 gather_fusion.4
  239.6 1.5 broadcast_select_fusion.1
  244.7 1.9 collective-permute-start.4
  248.0 2.0 collective-permute-start.6
  250.0 2.8 collective-permute-start.7
  255.8 3.2 scatter_custom_fusion.3
  259.0 3.2 scatter_custom_fusion.4
  262.1 3.2 scatter_custom_fusion.5
  265.3 3.2 scatter_custom_fusion.6
  268.5 106.7 %all-reduce.7.cloned.1.call-done = f32[549376]{0:T(1024)} async-done(((f32[549376]{0:T(1024)}), f32[549376]{0:T(1024)}) %all-reduce.7.cloned.1.call-update) | async-done | bytes 2197520 | tf_op jit(solution)/shard_map/psum | solution.py:256
  375.2 2.7 slice_multiply_fusion
  378.9 2.4 mul.316
  384.4 1.3 slice_multiply_fusion.3
  385.7 138.7 %all-reduce.9.cloned.1.call-done = f32[256,256]{1,0:T(8,128)} async-done(((f32[256,256]{1,0:T(8,128)}), f32[256,256]{1,0:T(8,128)}) %all-reduce.9.cloned.1.call-update) | async-done | bytes 262160 | tf_op jit(solution)/shard_map/psum | solution.py:269
  524.4 1.7 broadcast_multiply_fusion
  (160 shorter events, 31.1 us)
Async XLA Ops:
  7.2 128.8 %copy-start = (bf16[256,1024]{1,0:T(8,128)(2,1)S(1)}, bf16[256,1024]{1,0:T(8,128)(2,1)}, u32[]{:S(2)}) copy-start(bf16[256,1024]{1,0:T(8,128)(2,1)} %param.23) | copy-start | bytes 1572868
  7.2 7.3 %copy-start.2 = (s32[1,1024]{1,0:T(1,128)S(1)}, s32[1,1024]{1,0:T(1,128)}, u32[]{:S(2)}) copy-start(s32[1,1024]{1,0:T(1,128)} %param.15) | copy-start | bytes 12292
  14.5 4.6 copy-start.15
  19.0 13.8 %copy-start.31 = (s32[1,16,1024]{2,1,0:T(8,128)S(1)}, s32[1,16,1024]{2,1,0:T(8,128)}, u32[]{:S(2)}) copy-start(s32[1,16,1024]{2,1,0:T(8,128)} %param.18) | copy-start | bytes 196612
  20.4 35.5 %collective-permute-start = (bf16[64,256]{1,0:T(8,128)(2,1)S(1)}, bf16[64,256]{1,0:T(8,128)(2,1)S(1)}, u32[]{:S(2)}, u32[]{:S(2)}) collective-permute-start(bf16[64,256]{1,0:T(8,128)(2,1)S(1)} %get-tuple-element.62), channel_id=1, source_target_pairs={{32,0},{64,32},{96,64},{33,1},{65,33},{97,65},{34,2},{66,34},{98,6... | collective-permute-start | bytes 98312 | tf_op jit(solution)/shard_map/ppermute | solution.py:19
  21.7 34.2 %collective-permute-start.1 = (bf16[64,256]{1,0:T(8,128)(2,1)S(1)}, bf16[64,256]{1,0:T(8,128)(2,1)S(1)}, u32[]{:S(2)}, u32[]{:S(2)}) collective-permute-start(bf16[64,256]{1,0:T(8,128)(2,1)S(1)} %get-tuple-element.61), channel_id=1, source_target_pairs={{0,32},{32,64},{64,96},{1,33},{33,65},{65,97},{2,34},{34,66},{66,9... | collective-permute-start | bytes 98312 | tf_op jit(solution)/shard_map/ppermute | solution.py:19
  26.7 29.2 %collective-permute-start.2 = (bf16[64,256]{1,0:T(8,128)(2,1)S(1)}, bf16[64,256]{1,0:T(8,128)(2,1)S(1)}, u32[]{:S(2)}, u32[]{:S(2)}) collective-permute-start(bf16[64,256]{1,0:T(8,128)(2,1)S(1)} %get-tuple-element.60), channel_id=1, source_target_pairs={{1,0},{2,1},{3,2},{4,3},{5,4},{6,5},{7,6},{8,7},{9,8},{10,9},{11,1... | collective-permute-start | bytes 98312 | tf_op jit(solution)/shard_map/ppermute | solution.py:19
  29.6 26.3 %collective-permute-start.3 = (bf16[64,256]{1,0:T(8,128)(2,1)S(1)}, bf16[64,256]{1,0:T(8,128)(2,1)S(1)}, u32[]{:S(2)}, u32[]{:S(2)}) collective-permute-start(bf16[64,256]{1,0:T(8,128)(2,1)S(1)} %get-tuple-element.59), channel_id=1, source_target_pairs={{0,1},{1,2},{2,3},{3,4},{4,5},{5,6},{6,7},{7,8},{8,9},{9,10},{10,1... | collective-permute-start | bytes 98312 | tf_op jit(solution)/shard_map/ppermute | solution.py:19
  55.2 1.6 copy-start.3
  55.9 1.1 copy-start.29
  57.0 1.5 copy-start.25
  57.0 1.5 copy-start.27
  65.3 11.2 %copy-start.28 = (bf16[3,8,32,32]{3,2,1,0:T(8,128)(2,1)S(1)}, bf16[3,8,32,32]{3,2,1,0:T(8,128)(2,1)}, u32[]{:S(2)}) copy-start(bf16[3,8,32,32]{3,2,1,0:T(8,128)(2,1)} %param.21) | copy-start | bytes 147460
  65.3 41.7 %all-to-all-start = ((bf16[128,16,512]{2,1,0:T(8,128)(2,1)}), bf16[128,16,512]{2,1,0:T(8,128)(2,1)S(1)}, u32[]{:S(2)}, u32[]{:S(2)}) async-start(bf16[128,16,512]{2,1,0:T(8,128)(2,1)} %bitcast.148), calls=%async_computation | async-start | bytes 4194304 | tf_op jit(solution)/shard_map/all_to_all | solution.py:238
  77.8 5.7 %copy-start.33 = (s32[1,4,64]{2,1,0:T(4,128)S(1)}, s32[1,4,64]{2,1,0:T(4,128)}, u32[]{:S(2)}) copy-start(s32[1,4,64]{2,1,0:T(4,128)} %param.17) | copy-start | bytes 3076
  77.8 6.3 %copy-start.32 = (s32[1,2048]{1,0:T(1,128)S(1)}, s32[1,2048]{1,0:T(1,128)}, u32[]{:S(2)}) copy-start(s32[1,2048]{1,0:T(1,128)} %param.16) | copy-start | bytes 24580
  120.2 2.1 copy-start.35
  122.0 61.8 %copy-start.5 = (bf16[2048,512]{0,1:T(8,128)(2,1)}, bf16[2048,512]{0,1:T(8,128)(2,1)S(1)}, u32[]{:S(2)}) copy-start(bf16[2048,512]{0,1:T(8,128)(2,1)S(1)} %broadcast_select_fusion) | copy-start | bytes 6291460
  132.0 1.2 copy-start.13
  132.3 1.2 copy-start.24
  133.2 1.0 copy-start.14
  133.4 1.3 copy-start.10
  135.3 0.7 copy-start.34
  136.0 10.3 %copy-start.6 = (f32[2048,256]{0,1:T(8,128)}, f32[2048,256]{0,1:T(8,128)S(1)}, u32[]{:S(2)}) copy-start(f32[2048,256]{0,1:T(8,128)S(1)} %get-tuple-element.88) | copy-start | bytes 6291460
  136.0 1.4 copy-start.37
  137.5 6.5 %copy-start.12 = (f32[2048,1024]{1,0:T(8,128)}, f32[2048,1024]{1,0:T(8,128)S(1)}, u32[]{:S(2)}) copy-start(f32[2048,1024]{1,0:T(8,128)S(1)} %fusion.67) | copy-start | bytes 25165828
  148.9 5.3 copy-start.38
  154.2 7.7 %copy-start.22 = (f32[32,8,8,128]{3,2,1,0:T(8,128)S(1)}, f32[32,8,8,128]{3,2,1,0:T(8,128)}, u32[]{:S(2)}) copy-start(f32[32,8,8,128]{3,2,1,0:T(8,128)} %convolution_bitcast_fusion.1) | copy-start | bytes 3145732
  154.2 8.9 %copy-start.19 = (bf16[2048,256]{0,1:T(8,128)(2,1)S(1)}, bf16[2048,256]{0,1:T(8,128)(2,1)}, u32[]{:S(2)}) copy-start(bf16[2048,256]{0,1:T(8,128)(2,1)} %get-tuple-element.89) | copy-start | bytes 3145732
  161.9 2.0 copy-start.7
  180.1 3.6 copy-start.8
  180.1 3.6 copy-start.20
  183.8 1.4 copy-start.23
  199.5 35.0 %all-to-all-start.1 = ((bf16[128,16,512]{2,1,0:T(8,128)(2,1)}), bf16[128,16,512]{2,1,0:T(8,128)(2,1)S(1)}, u32[]{:S(2)}, u32[]{:S(2)}) async-start(bf16[128,16,512]{2,1,0:T(8,128)(2,1)} %bitcast.147), calls=%async_computation.1 | async-start | bytes 4194304 | tf_op jit(solution)/shard_map/all_to_all | solution.py:249
  203.9 171.3 %all-reduce.7.cloned.1.call-start = ((), (), s32[]{:S(2)}) async-start(), calls=%async_computation.2 | async-start | bytes 4399104 | tf_op jit(solution)/shard_map/psum | solution.py:256
  203.9 2.1 copy-start.9
  204.0 2.2 copy-start.17
  204.0 2.6 copy-start.11
  212.8 4.7 copy-start.16
  222.2 302.2 %all-reduce.9.cloned.1.call-start = ((), (), s32[]{:S(2)}) async-start(), calls=%async_computation.3 | async-start | bytes 524288 | tf_op jit(solution)/shard_map/psum | solution.py:269
  234.6 5.1 copy-start.36
  239.6 1.6 copy-start.21
  239.6 2.3 copy-start.30
  241.2 1.8 copy-start.4
  243.8 9.0 %copy-start.26 = (bf16[1024,256]{1,0:T(8,128)(2,1)S(1)}, bf16[1024,256]{1,0:T(8,128)(2,1)}, u32[]{:S(2)}) copy-start(bf16[1024,256]{1,0:T(8,128)(2,1)} %copy-done.25) | copy-start | bytes 1572868
  244.7 11.1 %collective-permute-start.4 = (bf16[64,256]{1,0:T(8,128)(2,1)S(1)}, bf16[64,256]{1,0:T(8,128)(2,1)S(1)}, u32[]{:S(2)}, u32[]{:S(2)}) collective-permute-start(bf16[64,256]{1,0:T(8,128)(2,1)S(1)} %get-tuple-element.58), channel_id=1, source_target_pairs={{0,32},{32,64},{64,96},{1,33},{33,65},{65,97},{2,34},{34,66},{66,9... | collective-permute-start | bytes 98312 | tf_op jit(solution)/shard_map/ppermute | solution.py:19
  246.7 12.3 %collective-permute-start.5 = (bf16[64,256]{1,0:T(8,128)(2,1)S(1)}, bf16[64,256]{1,0:T(8,128)(2,1)S(1)}, u32[]{:S(2)}, u32[]{:S(2)}) collective-permute-start(bf16[64,256]{1,0:T(8,128)(2,1)S(1)} %get-tuple-element.57), channel_id=1, source_target_pairs={{32,0},{64,32},{96,64},{33,1},{65,33},{97,65},{34,2},{66,34},{98,6... | collective-permute-start | bytes 98312 | tf_op jit(solution)/shard_map/ppermute | solution.py:19
  248.0 14.2 %collective-permute-start.6 = (bf16[64,256]{1,0:T(8,128)(2,1)S(1)}, bf16[64,256]{1,0:T(8,128)(2,1)S(1)}, u32[]{:S(2)}, u32[]{:S(2)}) collective-permute-start(bf16[64,256]{1,0:T(8,128)(2,1)S(1)} %get-tuple-element.56), channel_id=1, source_target_pairs={{0,1},{1,2},{2,3},{3,4},{4,5},{5,6},{6,7},{7,8},{8,9},{9,10},{10,1... | collective-permute-start | bytes 98312 | tf_op jit(solution)/shard_map/ppermute | solution.py:19
  250.0 15.3 %collective-permute-start.7 = (bf16[64,256]{1,0:T(8,128)(2,1)S(1)}, bf16[64,256]{1,0:T(8,128)(2,1)S(1)}, u32[]{:S(2)}, u32[]{:S(2)}) collective-permute-start(bf16[64,256]{1,0:T(8,128)(2,1)S(1)} %get-tuple-element.55), channel_id=1, source_target_pairs={{1,0},{2,1},{3,2},{4,3},{5,4},{6,5},{7,6},{8,7},{9,8},{10,9},{11,1... | collective-permute-start | bytes 98312 | tf_op jit(solution)/shard_map/ppermute | solution.py:19
  378.9 3.7 copy-start.18
  381.3 144.7 %copy-start.1 = (bf16[256,1024]{1,0:T(8,128)(2,1)S(1)}, bf16[256,1024]{1,0:T(8,128)(2,1)}, u32[]{:S(2)}) copy-start(bf16[256,1024]{1,0:T(8,128)(2,1)} %param.23) | copy-start | bytes 1572868
Sparse Core Ops, SparseCore 0:
  222.3 152.8 all-reduce.6
  384.5 139.8 all-reduce.8
